TPU v7x, 256 devices: a whole 4x4x8 slice. The times are simulated.
256 devices in a mesh: pipe: 4 (over y), req: 16 (over z, core), tp: 4 (over x).
Axes of the slice: x: 4, y: 4, z: 8, core: 2. Of those that a mesh axis runs over, the one named last changes fastest.
Arguments:
- hidden: bfloat16 [2048, 8192], P('req', 'tp'), may hold values from -64 to 64
- queries: bfloat16 [4, 2048, 4096], P('pipe', 'req', 'tp'), may hold values from -32 to 32
- norm_gain: bfloat16 [4, 8192], P('pipe'), may hold values from 0.5 to 1.5
- kv_weight: bfloat16 [4, 8192, 2, 512], P('pipe', None, None, 'tp'), may hold values from -0.0625 to 0.0625
- adapter_in: bfloat16 [4, 64, 64, 4096], P('pipe', 'req', None, 'tp'), may hold values from -0.09375 to 0.09375
- adapter_out: bfloat16 [4, 64, 64, 8192], P('pipe', 'req', None, 'tp'), may hold values from -3 to 3
- kv_pages: bfloat16 [4, 2048, 2, 64, 512], P('pipe', 'req', None, None, 'tp'), may hold values from -4 to 4
- adapter_ids: int32 [512], P('req'), may hold values from 0 to 63, as said below
- owner_rows: int32 [64], replicated, may hold values from 0 to 63, as said below
- page_table: int32 [512, 4], P('req'), may hold values from 0 to 127, as said below
- lengths: int32 [512], P('req'), may hold values from 1 to 252, as said below
- moves: int32 [256, 3], P('req'), may hold values from 0 to 127, as said below
Outputs:
- section_out: bfloat16 [4, 2048, 8192], P('pipe', 'req', 'tp')
- new_kv: bfloat16 [4, 2048, 2, 512], P('pipe', 'req', None, 'tp')
- arrived: bfloat16 [4, 480, 2, 64, 512], P('pipe', 'req', None, None, 'tp')
Inputs may be any that keep to these rules, and one draw needn't show every extreme that they name: `adapter_ids`: adapter a is stored at row owner_rows[a], on request device owner_rows[a] // 4. In each aligned block of 16 requests at most 2 requests have adapters stored on one request device, and in every block some device stores exactly 2 of them. `owner_rows`: each storage row once. `page_table`: the 128 slots of one request device are each named once by its requests. `lengths`: every request device has a request of length 252. `moves`: row i * 16 + k belongs to request device i. Its destination differs from i; its source slots are distinct; at most 2 of its rows name one destination, exactly 2 for some; destination slots are below 30 and distinct among all rows that name one destination.
All inputs are finite; a program needn't handle non-finite values.
Results may differ from a plain program's by a relative error of at most 0.02.
Values may be sent and summed in bfloat16 or wider, within the bound.
A program may use at most 128 MiB of HBM per device.

v0:
```python
import math

import jax
import jax.numpy as jnp
from jax import lax
from jax.sharding import PartitionSpec as P

D = 8192
HD = 128
R = 64
ADP_DEV = 4
RQ = 32
S = 4
MICRO = 2
PAGE = 64
MOVES = 16
RQ_MB = 16
CTX = 256


def passed_along(block, axis, distance):
    devices = range(lax.axis_size(axis))
    route = [(i - distance, i) for i in devices if i - distance in devices]
    return lax.ppermute(block, axis, route)


def rotate(key_vecs, positions):
    half_dim = key_vecs.shape[-1] // 2
    inv_freq = jnp.exp(
        -math.log(500000.0) * (2.0 * jnp.arange(half_dim, dtype=jnp.float32) / key_vecs.shape[-1])
    )
    angles = positions.astype(jnp.float32)[..., None, None] * inv_freq
    cos_vals = jnp.cos(angles)
    sin_vals = jnp.sin(angles)
    front_half = key_vecs[..., :half_dim]
    back_half = key_vecs[..., half_dim:]
    return jnp.concatenate(
        [
            front_half * cos_vals - back_half * sin_vals,
            back_half * cos_vals + front_half * sin_vals,
        ],
        axis=-1,
    )


def body(
    hidden,
    queries,
    norm_gain,
    kv_weight,
    adapter_in,
    adapter_out,
    kv_pages,
    adapter_ids,
    owner_rows,
    page_table,
    lengths,
    moves,
):
    section_count = lax.axis_size("pipe")
    req_count = lax.axis_size("req")
    section_id = lax.axis_index("pipe")
    my_req = lax.axis_index("req")
    width_loc = hidden.shape[1]
    q_width = queries.shape[2]
    kv_width = kv_weight.shape[3]
    kv_heads = kv_width // HD
    group_size = q_width // HD // kv_heads
    batches = 1
    per_batch = RQ // batches
    rows_per = per_batch * S
    block_cap = min(RQ_MB, max(2, 2 * RQ_MB // req_count))
    batch_cap = block_cap * (MICRO // batches)
    pair_cap = (MOVES + req_count - 2) // (req_count - 1)
    free_slots = (req_count - 1) * pair_cap
    token_ids = jnp.arange(S, dtype=jnp.int32)
    store_rows = owner_rows[adapter_ids]
    dest_all = store_rows // ADP_DEV
    pick_all = store_rows % ADP_DEV
    req_ids = jnp.arange(RQ, dtype=jnp.int32)
    earlier = (
        (req_ids[None, :] < req_ids[:, None])
        & (req_ids[None, :] // per_batch == req_ids[:, None] // per_batch)
        & (dest_all[None, :] == dest_all[:, None])
    )
    slot_all = jnp.sum(earlier.astype(jnp.int32), axis=1)
    positions = (lengths[:, None] + token_ids[None, :]).reshape(RQ * S)
    gain_full = norm_gain[0].astype(jnp.float32)
    weight_flat = kv_weight[0].reshape(D, 2 * kv_width)
    layer_pages = kv_pages[0]
    adapters_in = adapter_in[0]
    adapters_out = adapter_out[0].reshape(ADP_DEV * R, width_loc)
    key_pos = jnp.arange(CTX, dtype=jnp.int32)
    causal = token_ids[None, :] <= token_ids[:, None]
    adapter_slots = jnp.arange(ADP_DEV, dtype=jnp.int32)
    carried = jnp.zeros((rows_per, width_loc), jnp.bfloat16)
    section_rows = jnp.zeros((RQ * S, width_loc), jnp.bfloat16)
    fresh_rows = jnp.zeros((RQ * S, 2, kv_width), jnp.bfloat16)
    for tick_id in range(batches + section_count - 1):
        offset_batch = tick_id - section_id
        active = (offset_batch >= 0) & (offset_batch < batches)
        hstate = jnp.where(section_id == 0, hidden, carried)
        whole_rows = lax.all_gather(hstate, "tp", axis=1, tiled=True)
        widened = whole_rows.astype(jnp.float32)
        inv_rms = lax.rsqrt(jnp.mean(widened * widened, axis=-1, keepdims=True) + 1e-05)
        normed = (widened * inv_rms * gain_full).astype(jnp.bfloat16)
        projected = jnp.dot(normed, weight_flat, preferred_element_type=jnp.float32).reshape(
            rows_per, 2, kv_heads, HD
        )
        new_keys = rotate(projected[:, 0], positions).astype(jnp.bfloat16)
        new_values = projected[:, 1].astype(jnp.bfloat16)
        fresh_kv = jnp.stack(
            [new_keys.reshape(rows_per, kv_width), new_values.reshape(rows_per, kv_width)], axis=1
        )
        gathered = layer_pages[page_table]
        cached = jnp.swapaxes(gathered, 1, 2).reshape(per_batch, 2, CTX, kv_heads, HD)
        fresh_heads = fresh_kv.reshape(per_batch, S, 2, kv_heads, HD)
        query_heads = queries[0].reshape(per_batch, S, kv_heads, group_size, HD)
        score_old = jnp.einsum(
            "bskgd,btkd->bskgt", query_heads, cached[:, 0], preferred_element_type=jnp.float32
        ) * HD ** (-0.5)
        score_new = jnp.einsum(
            "bskgd,btkd->bskgt",
            query_heads,
            fresh_heads[:, :, 0],
            preferred_element_type=jnp.float32,
        ) * HD ** (-0.5)
        old_ok = key_pos[None, :] < lengths[:, None]
        score_old = jnp.where(old_ok[:, None, None, None, :], score_old, -jnp.inf)
        score_new = jnp.where(causal[None, :, None, None, :], score_new, -jnp.inf)
        row_max = jnp.maximum(jnp.max(score_old, axis=-1), jnp.max(score_new, axis=-1))[..., None]
        exp_old = jnp.exp(score_old - row_max)
        exp_new = jnp.exp(score_new - row_max)
        denominator = (jnp.sum(exp_old, axis=-1) + jnp.sum(exp_new, axis=-1))[..., None]
        weight_old = (exp_old / denominator).astype(jnp.bfloat16)
        weight_new = (exp_new / denominator).astype(jnp.bfloat16)
        mixed = jnp.einsum(
            "bskgt,btkd->bskgd", weight_old, cached[:, 1], preferred_element_type=jnp.float32
        )
        mixed = mixed + jnp.einsum(
            "bskgt,btkd->bskgd",
            weight_new,
            fresh_heads[:, :, 1],
            preferred_element_type=jnp.float32,
        )
        attended = mixed.reshape(per_batch, S, q_width).astype(jnp.bfloat16)
        outgoing = (
            jnp.zeros((req_count, batch_cap, S, q_width), jnp.bfloat16)
            .at[dest_all, slot_all]
            .set(attended)
        )
        picks_out = (
            jnp.zeros((req_count, batch_cap), jnp.int32).at[dest_all, slot_all].set(pick_all)
        )
        rows_in = lax.all_to_all(outgoing, "req", split_axis=0, concat_axis=0, tiled=True)
        picks_in = lax.all_to_all(picks_out, "req", split_axis=0, concat_axis=0, tiled=True)
        sources = rows_in.shape[0]
        item_count = rows_in.shape[1]
        flat_rows = rows_in.reshape(sources * item_count * S, q_width)
        all_low = jnp.einsum(
            "nf,arf->nar", flat_rows, adapters_in, preferred_element_type=jnp.float32
        )
        picks_rows = jnp.broadcast_to(picks_in[:, :, None], (sources, item_count, S)).reshape(
            sources * item_count * S
        )
        one_hot = (picks_rows[:, None] == adapter_slots[None, :]).astype(jnp.float32)
        partial_low = jnp.sum(all_low * one_hot[:, :, None], axis=1)
        rank_low = lax.psum(partial_low, "tp").astype(jnp.bfloat16)
        spread = (rank_low.astype(jnp.float32)[:, None, :] * one_hot[:, :, None]).astype(
            jnp.bfloat16
        )
        deltas = jnp.dot(
            spread.reshape(sources * item_count * S, ADP_DEV * R),
            adapters_out,
            preferred_element_type=jnp.float32,
        ).astype(jnp.bfloat16)
        deltas = deltas.reshape(sources, item_count, S, width_loc)
        returned = lax.all_to_all(deltas, "req", split_axis=0, concat_axis=0, tiled=True)
        delta_rows = returned[dest_all, slot_all].reshape(rows_per, width_loc)
        new_state = (hstate.astype(jnp.float32) + delta_rows.astype(jnp.float32)).astype(
            jnp.bfloat16
        )
        section_rows = jnp.where(active, new_state, section_rows)
        fresh_rows = jnp.where(active, fresh_kv, fresh_rows)
        carried = passed_along(new_state, "pipe", 1)
    page_slot = jnp.take_along_axis(page_table, (positions // PAGE).reshape(RQ, S), axis=1).reshape(
        RQ * S
    )
    written = layer_pages.at[page_slot, :, positions % PAGE, :].set(fresh_rows)
    leaving = written[moves[:, 1]]
    empty_pages = jnp.zeros((free_slots, 2, PAGE, kv_width), jnp.bfloat16)
    received, dest_in, spots_in = (
        lax.all_gather(leaving, "req", axis=0, tiled=True),
        lax.all_gather(moves[:, 0], "req", axis=0, tiled=True),
        lax.all_gather(moves[:, 2], "req", axis=0, tiled=True),
    )
    target = jnp.where(dest_in == my_req, spots_in, free_slots)
    arrived = empty_pages.at[target].set(received, mode="drop")
    return (section_rows[None], fresh_rows[None], arrived[None])


def solution(mesh):
    in_specs = (
        P("req", "tp"),
        P("pipe", "req", "tp"),
        P("pipe", None),
        P("pipe", None, None, "tp"),
        P("pipe", "req", None, "tp"),
        P("pipe", "req", None, "tp"),
        P("pipe", "req", None, None, "tp"),
        P("req"),
        P(),
        P("req", None),
        P("req"),
        P("req", None),
    )
    out_specs = (
        P("pipe", "req", "tp"),
        P("pipe", "req", None, "tp"),
        P("pipe", "req", None, None, "tp"),
    )
    return jax.shard_map(body, mesh=mesh, in_specs=in_specs, out_specs=out_specs, check_vma=False)
```

profile of v0, /device:TPU:8, one launch (start us, length us, event | category | flops | bytes accessed | tf_op | source)
XLA Modules:
  0.0 678.1 jit_solution(13110023166063998771)
XLA Ops:
  13.1 8.6 %all-to-all-start.1 = ((s32[16,1,4]{2,1,0:T(1,128)}), s32[16,1,4]{2,1,0:T(1,128)S(1)}, u32[]{:S(2)}, u32[]{:S(2)}) async-start(s32[16,1,4]{2,1,0:T(1,128)} %copy.87), calls=%async_computation.1 | async-start | bytes 16384 | tf_op jit(solution)/shard_map/all_to_all | solution.py:156
  33.1 12.7 %copy.118 = bf16[1,128,2,64,128]{4,2,3,1,0:T(2,128)(2,1)} copy(bf16[1,128,2,64,128]{4,3,2,1,0:T(8,128)(2,1)} %param.18) | data formatting | bytes 8388608 | tf_op args[6]
  46.1 14.3 %gather_fusion.1 = bf16[128,2,64,128]{3,1,2,0:T(2,128)(2,1)} fusion(bf16[128,2,64,128]{3,1,2,0:T(2,128)(2,1)} %bitcast.354, s32[1024]{0:T(1024)S(1)} %pad_clamp_fusion.1), kind=kCustom, calls=%fused_computation.1 | custom fusion | bytes 8389120 | tf_op jit(solution)/shard_map/gather | solution.py:115
  93.1 15.8 %all-to-all-done = bf16[16,4,4,1024]{3,2,1,0:T(4,128)(2,1)S(1)} async-done(((bf16[16,4,4,1024]{3,2,1,0:T(4,128)(2,1)}), bf16[16,4,4,1024]{3,2,1,0:T(4,128)(2,1)S(1)}, u32[]{:S(2)}, u32[]{:S(2)}) %all-to-all-start) | async-done | bytes 524320 | tf_op jit(solution)/shard_map/all_to_all | solution.py:155
  110.4 17.6 %psum.28 = bf16[256,64]{0,1:T(8,128)(2,1)S(1)} all-reduce(f32[256,64]{0,1:T(8,128)S(1)} %fusion.53), channel_id=1, replica_groups=mesh['pipe'=4,'req'=16,'tp'=4] {'tp'}, use_global_device_ids=true, to_apply=%region_9.10 | all-reduce | flops 16384 | bytes 98304 | tf_op jit(solution)/shard_map/psum | solution.py:168
  131.7 31.5 %all_to_all.52 = bf16[16,4,4,2048]{3,2,1,0:T(4,128)(2,1)} all-to-all(bf16[16,4,4,2048]{3,2,1,0:T(4,128)(2,1)} %reshape.1462), channel_id=1, replica_groups=mesh['pipe'=4,'req'=16,'tp'=4] {'req'}, dimensions={0} | all-to-all | bytes 2097152 | tf_op jit(solution)/shard_map/all_to_all | solution.py:178
  172.3 12.5 %collective-permute-done = bf16[128,2048]{1,0:T(8,128)(2,1)S(1)} collective-permute-done((bf16[128,2048]{1,0:T(8,128)(2,1)S(1)}, bf16[128,2048]{1,0:T(8,128)(2,1)S(1)}, u32[]{:S(2)}, u32[]{:S(2)}) %collective-permute-start) | collective-permute-done | bytes 524320 | tf_op jit(solution)/shard_map/ppermute | solution.py:24
  185.7 10.8 %all-gather.13.cloned.1.call-start = ((), (), s32[]{:S(2)}) async-start(), calls=%async_computation.11 | async-start | bytes 2621440 | tf_op jit(solution)/shard_map/all_gather | solution.py:103
  196.5 19.5 %all-gather.11.cloned.1.call-done = bf16[128,8192]{1,0:T(8,128)(2,1)} async-done(((bf16[128,2048]{1,0:T(8,128)(2,1)}), bf16[128,8192]{1,0:T(8,128)(2,1)}) %all-gather.11.cloned.1.call-update) | async-done | bytes 2097168 | tf_op jit(solution)/shard_map/all_gather | solution.py:103
  232.9 23.0 %all_to_all.53 = bf16[16,4,4,1024]{3,2,1,0:T(4,128)(2,1)} all-to-all(bf16[16,4,4,1024]{3,2,1,0:T(4,128)(2,1)S(1)} %scatter_fusion.2), channel_id=1, replica_groups=mesh['pipe'=4,'req'=16,'tp'=4] {'req'}, dimensions={0} | all-to-all | bytes 1048576 | tf_op jit(solution)/shard_map/all_to_all | solution.py:155
  258.6 15.6 %psum.29 = bf16[256,64]{0,1:T(8,128)(2,1)S(1)} all-reduce(f32[256,64]{0,1:T(8,128)S(1)} %fusion.54), channel_id=1, replica_groups=mesh['pipe'=4,'req'=16,'tp'=4] {'tp'}, use_global_device_ids=true, to_apply=%region_16.17 | all-reduce | flops 16384 | bytes 98304 | tf_op jit(solution)/shard_map/psum | solution.py:168
  278.0 31.5 %all_to_all.54 = bf16[16,4,4,2048]{3,2,1,0:T(4,128)(2,1)} all-to-all(bf16[16,4,4,2048]{3,2,1,0:T(4,128)(2,1)} %reshape.1466), channel_id=1, replica_groups=mesh['pipe'=4,'req'=16,'tp'=4] {'req'}, dimensions={0} | all-to-all | bytes 2097152 | tf_op jit(solution)/shard_map/all_to_all | solution.py:178
  320.3 12.6 %collective-permute-done.1 = bf16[128,2048]{1,0:T(8,128)(2,1)S(1)} collective-permute-done((bf16[128,2048]{1,0:T(8,128)(2,1)S(1)}, bf16[128,2048]{1,0:T(8,128)(2,1)S(1)}, u32[]{:S(2)}, u32[]{:S(2)}) %collective-permute-start.1) | collective-permute-done | bytes 524320 | tf_op jit(solution)/shard_map/ppermute | solution.py:24
  333.8 30.2 %all-gather.13.cloned.1.call-done = bf16[128,8192]{1,0:T(8,128)(2,1)} async-done(((bf16[128,2048]{1,0:T(8,128)(2,1)}), bf16[128,8192]{1,0:T(8,128)(2,1)}) %all-gather.13.cloned.1.call-update) | async-done | bytes 2097168 | tf_op jit(solution)/shard_map/all_gather | solution.py:103
  382.1 23.1 %all_to_all.55 = bf16[16,4,4,1024]{3,2,1,0:T(4,128)(2,1)} all-to-all(bf16[16,4,4,1024]{3,2,1,0:T(4,128)(2,1)S(1)} %scatter_fusion.3), channel_id=1, replica_groups=mesh['pipe'=4,'req'=16,'tp'=4] {'req'}, dimensions={0} | all-to-all | bytes 1048576 | tf_op jit(solution)/shard_map/all_to_all | solution.py:155
  407.7 15.7 %psum.30 = bf16[256,64]{0,1:T(8,128)(2,1)S(1)} all-reduce(f32[256,64]{0,1:T(8,128)S(1)} %fusion.55), channel_id=1, replica_groups=mesh['pipe'=4,'req'=16,'tp'=4] {'tp'}, use_global_device_ids=true, to_apply=%region_23.24 | all-reduce | flops 16384 | bytes 98304 | tf_op jit(solution)/shard_map/psum | solution.py:168
  427.1 31.7 %all_to_all.56 = bf16[16,4,4,2048]{3,2,1,0:T(4,128)(2,1)} all-to-all(bf16[16,4,4,2048]{3,2,1,0:T(4,128)(2,1)} %reshape.1470), channel_id=1, replica_groups=mesh['pipe'=4,'req'=16,'tp'=4] {'req'}, dimensions={0} | all-to-all | bytes 2097152 | tf_op jit(solution)/shard_map/all_to_all | solution.py:178
  469.5 12.6 %collective-permute-done.2 = bf16[128,2048]{1,0:T(8,128)(2,1)S(1)} collective-permute-done((bf16[128,2048]{1,0:T(8,128)(2,1)S(1)}, bf16[128,2048]{1,0:T(8,128)(2,1)S(1)}, u32[]{:S(2)}, u32[]{:S(2)}) %collective-permute-start.2) | collective-permute-done | bytes 524320 | tf_op jit(solution)/shard_map/ppermute | solution.py:24
  488.4 24.7 %all-gather.15.cloned.1.call-done = bf16[128,8192]{1,0:T(8,128)(2,1)} async-done(((bf16[128,2048]{1,0:T(8,128)(2,1)}), bf16[128,8192]{1,0:T(8,128)(2,1)}) %all-gather.15.cloned.1.call-update) | async-done | bytes 2097168 | tf_op jit(solution)/shard_map/all_gather | solution.py:103
  520.0 15.6 %scatter_fusion.5 = bf16[128,2,64,128]{3,1,2,0:T(2,128)(2,1)} fusion(bf16[128,2,64,128]{3,1,2,0:T(2,128)(2,1)} %bitcast.355, s32[128]{0:T(128)S(1)} %fusion.154, bf16[128,2,128]{2,1,0:T(2,128)(2,1)S(1)} %copy.99), kind=kCustom, calls=%fused_computation.13 | custom fusion | bytes 197632 | tf_op jit(solution)/shard_map/scatter | solution.py:189
  560.1 20.8 %all-to-all-done.7 = bf16[16,4,4,1024]{3,2,1,0:T(4,128)(2,1)S(1)} async-done(((bf16[16,4,4,1024]{3,2,1,0:T(4,128)(2,1)}), bf16[16,4,4,1024]{3,2,1,0:T(4,128)(2,1)S(1)}, u32[]{:S(2)}, u32[]{:S(2)}) %all-to-all-start.7) | async-done | bytes 524320 | tf_op jit(solution)/shard_map/all_to_all | solution.py:155
  582.4 15.6 %psum.31 = bf16[256,64]{0,1:T(8,128)(2,1)S(1)} all-reduce(f32[256,64]{0,1:T(8,128)S(1)} %fusion.56), channel_id=1, replica_groups=mesh['pipe'=4,'req'=16,'tp'=4] {'tp'}, use_global_device_ids=true, to_apply=%region_30.31 | all-reduce | flops 16384 | bytes 98304 | tf_op jit(solution)/shard_map/psum | solution.py:168
  604.1 33.5 %all-reduce.2 = (s32[256]{0:T(256)S(1)}, s32[256]{0:T(256)S(1)}) all-reduce(s32[256]{0:T(256)S(1)} %bitcast_dynamic-update-slice_fusion, s32[256]{0:T(256)S(1)} %bitcast_dynamic-update-slice_fusion.1), channel_id=3, replica_groups=mesh['pipe'=4,'req'=16,'tp'=4] {'req'}, use_global_device_ids=true, to_apply=%add.1 | all-reduce | flops 512 | bytes 4096
  646.3 24.0 %scatter_fusion.6 = bf16[30,2,64,128]{3,2,1,0:T(8,128)(2,1)S(1)} fusion(bf16[30,2,64,128]{3,2,1,0:T(8,128)(2,1)S(1)} %broadcast_in_dim.90, s32[256]{0:T(256)S(1)} %compare_select_fusion.2, bf16[256,2,64,128]{3,2,1,0:T(8,128)(2,1)} %all-gather.17.cloned.1.call-done), kind=kCustom, calls=%fused_computation.14 | custom fusion | bytes 25166848 | tf_op jit(solution)/shard_map/scatter | solution.py:198
  (287 shorter events, 188.6 us)
Async XLA Ops:
  7.2 120.8 %copy-start = (bf16[1,4,64,2048]{3,2,1,0:T(8,128)(2,1)S(1)}, bf16[1,4,64,2048]{3,2,1,0:T(8,128)(2,1)}, u32[]{:S(2)}) copy-start(bf16[1,4,64,2048]{3,2,1,0:T(8,128)(2,1)} %param.17) | copy-start | bytes 3145732
  7.2 59.4 %all-gather.9.cloned.1.call-start = ((), (), s32[]{:S(2)}) async-start(), calls=%async_computation.9 | async-start | bytes 2621440 | tf_op jit(solution)/shard_map/all_gather | solution.py:103
  13.1 72.5 %all-to-all-start.1 = ((s32[16,1,4]{2,1,0:T(1,128)}), s32[16,1,4]{2,1,0:T(1,128)S(1)}, u32[]{:S(2)}, u32[]{:S(2)}) async-start(s32[16,1,4]{2,1,0:T(1,128)} %copy.87), calls=%async_computation.1 | async-start | bytes 16384 | tf_op jit(solution)/shard_map/all_to_all | solution.py:156
  32.9 185.2 %copy-start.27 = (f32[1,8192]{1,0:T(1,128)}, f32[1,8192]{1,0:T(1,128)S(1)}, u32[]{:S(2)}) copy-start(f32[1,8192]{1,0:T(1,128)S(1)} %mul.401) | copy-start | bytes 98308
  33.0 39.8 %copy-start.30 = (f32[128]{0:T(128)}, f32[128]{0:T(128)S(1)}, u32[]{:S(2)}) copy-start(f32[128]{0:T(128)S(1)} %convert_element_type.449) | copy-start | bytes 1540
  33.1 40.2 %copy-start.17 = (bf16[16,8,8,128]{3,2,1,0:T(8,128)(2,1)}, bf16[16,8,8,128]{3,2,1,0:T(8,128)(2,1)S(1)}, u32[]{:S(2)}) copy-start(bf16[16,8,8,128]{3,2,1,0:T(8,128)(2,1)S(1)} %copy.113) | copy-start | bytes 786436
  85.6 23.3 %all-to-all-start = ((bf16[16,4,4,1024]{3,2,1,0:T(4,128)(2,1)}), bf16[16,4,4,1024]{3,2,1,0:T(4,128)(2,1)S(1)}, u32[]{:S(2)}, u32[]{:S(2)}) async-start(bf16[16,4,4,1024]{3,2,1,0:T(4,128)(2,1)} %scatter_fusion), calls=%async_computation | async-start | bytes 1048576 | tf_op jit(solution)/shard_map/all_to_all | solution.py:155
  92.8 123.2 %all-gather.11.cloned.1.call-start = ((), (), s32[]{:S(2)}) async-start(), calls=%async_computation.10 | async-start | bytes 2621440 | tf_op jit(solution)/shard_map/all_gather | solution.py:103
  128.0 38.7 %copy-start.3 = (bf16[128,2048]{1,0:T(8,128)(2,1)S(1)}, bf16[128,2048]{1,0:T(8,128)(2,1)}, u32[]{:S(2)}) copy-start(bf16[128,2048]{1,0:T(8,128)(2,1)} %param.12) | copy-start | bytes 1572868
  168.8 16.0 %collective-permute-start = (bf16[128,2048]{1,0:T(8,128)(2,1)S(1)}, bf16[128,2048]{1,0:T(8,128)(2,1)S(1)}, u32[]{:S(2)}, u32[]{:S(2)}) collective-permute-start(bf16[128,2048]{1,0:T(8,128)(2,1)S(1)} %add_convert_fusion.3), channel_id=1, source_target_pairs={{0,64},{64,128},{128,192},{1,65},{65,129},{129,193},{2,66},{66,130... | collective-permute-start | bytes 1572872 | tf_op jit(solution)/shard_map/ppermute | solution.py:24
  185.7 178.3 %all-gather.13.cloned.1.call-start = ((), (), s32[]{:S(2)}) async-start(), calls=%async_computation.11 | async-start | bytes 2621440 | tf_op jit(solution)/shard_map/all_gather | solution.py:103
  274.3 40.5 %copy-start.5 = (bf16[128,2048]{1,0:T(8,128)(2,1)S(1)}, bf16[128,2048]{1,0:T(8,128)(2,1)}, u32[]{:S(2)}) copy-start(bf16[128,2048]{1,0:T(8,128)(2,1)} %broadcast_select_fusion.2) | copy-start | bytes 1572868
  312.5 53.5 %copy-start.28 = (f32[1,8192]{1,0:T(1,128)S(1)}, f32[1,8192]{1,0:T(1,128)}, u32[]{:S(2)}) copy-start(f32[1,8192]{1,0:T(1,128)} %copy-done.27) | copy-start | bytes 98308
  316.9 16.0 %collective-permute-start.1 = (bf16[128,2048]{1,0:T(8,128)(2,1)S(1)}, bf16[128,2048]{1,0:T(8,128)(2,1)S(1)}, u32[]{:S(2)}, u32[]{:S(2)}) collective-permute-start(bf16[128,2048]{1,0:T(8,128)(2,1)S(1)} %add_convert_fusion.2), channel_id=1, source_target_pairs={{0,64},{64,128},{128,192},{1,65},{65,129},{129,193},{2,66},{66,130... | collective-permute-start | bytes 1572872 | tf_op jit(solution)/shard_map/ppermute | solution.py:24
  333.7 179.5 %all-gather.15.cloned.1.call-start = ((), (), s32[]{:S(2)}) async-start(), calls=%async_computation.12 | async-start | bytes 2621440 | tf_op jit(solution)/shard_map/all_gather | solution.py:103
  423.4 40.6 %copy-start.6 = (bf16[128,2048]{1,0:T(8,128)(2,1)S(1)}, bf16[128,2048]{1,0:T(8,128)(2,1)}, u32[]{:S(2)}) copy-start(bf16[128,2048]{1,0:T(8,128)(2,1)} %broadcast_select_fusion.1) | copy-start | bytes 1572868
  427.1 56.1 %copy-start.39 = (s32[32]{0:T(128)S(1)}, s32[32]{0:T(128)}, u32[]{:S(2)}) copy-start(s32[32]{0:T(128)} %param.22) | copy-start | bytes 388
  466.1 16.0 %collective-permute-start.2 = (bf16[128,2048]{1,0:T(8,128)(2,1)S(1)}, bf16[128,2048]{1,0:T(8,128)(2,1)S(1)}, u32[]{:S(2)}, u32[]{:S(2)}) collective-permute-start(bf16[128,2048]{1,0:T(8,128)(2,1)S(1)} %add_convert_fusion.1), channel_id=1, source_target_pairs={{0,64},{64,128},{128,192},{1,65},{65,129},{129,193},{2,66},{66,130... | collective-permute-start | bytes 1572872 | tf_op jit(solution)/shard_map/ppermute | solution.py:24
  483.0 163.1 %all-gather.17.cloned.1.call-start = ((), (), s32[]{:S(2)}) async-start(), calls=%async_computation.13 | async-start | bytes 8912896 | tf_op jit(solution)/shard_map/all_gather | solution.py:193
  483.4 31.9 %copy-start.29 = (f32[1,8192]{1,0:T(1,128)S(1)}, f32[1,8192]{1,0:T(1,128)}, u32[]{:S(2)}) copy-start(f32[1,8192]{1,0:T(1,128)} %copy-done.27) | copy-start | bytes 98308
  551.8 29.0 %all-to-all-start.7 = ((bf16[16,4,4,1024]{3,2,1,0:T(4,128)(2,1)}), bf16[16,4,4,1024]{3,2,1,0:T(4,128)(2,1)S(1)}, u32[]{:S(2)}, u32[]{:S(2)}) async-start(bf16[16,4,4,1024]{3,2,1,0:T(4,128)(2,1)} %scatter_fusion.4), calls=%async_computation.7 | async-start | bytes 1048576 | tf_op jit(solution)/shard_map/all_to_all | solution.py:155
  598.5 45.4 %copy-start.4 = (bf16[128,2048]{1,0:T(8,128)(2,1)S(1)}, bf16[128,2048]{1,0:T(8,128)(2,1)}, u32[]{:S(2)}) copy-start(bf16[128,2048]{1,0:T(8,128)(2,1)} %broadcast_select_fusion) | copy-start | bytes 1572868
  598.5 45.4 %copy-start.9 = (bf16[128,2048]{1,0:T(8,128)(2,1)S(1)}, bf16[128,2048]{1,0:T(8,128)(2,1)}, u32[]{:S(2)}) copy-start(bf16[128,2048]{1,0:T(8,128)(2,1)} %copy-done.8) | copy-start | bytes 1572868
  599.8 41.2 %all-to-all-start.8 = ((bf16[16,4,4,2048]{3,2,1,0:T(4,128)(2,1)}), bf16[16,4,4,2048]{3,2,1,0:T(4,128)(2,1)S(1)}, u32[]{:S(2)}, u32[]{:S(2)}) async-start(bf16[16,4,4,2048]{3,2,1,0:T(4,128)(2,1)} %reshape.1474), calls=%async_computation.8 | async-start | bytes 2097152 | tf_op jit(solution)/shard_map/all_to_all | solution.py:178
  (32 other events, 227.1 us)
Sparse Core Ops, SparseCore 0:
  10.4 36.2 all-gather.8
  185.8 30.1 all-gather.10
  333.8 30.0 all-gather.12
  483.1 30.0 all-gather.14
  540.6 67.0 all-gather.16
where the time goes:
time: 690 us; the launch traced here: 678 us
  blocking collectives  239 us (35%)
  local copies, waits for them, and re-layouts  150 us (22%)
  waiting for transfers between devices  149 us (22%)
  matrix products  51.9 us (8%)
  starting transfers between devices  48.2 us (7%)
  other arithmetic  24.4 us (4%)
  between operations  16.3 us (2%)
    all_to_all x3, blocking collectives, body(): lax.all_to_all(deltas, 'req', split_axis=0, concat_axis=0, tiled=True)  94.7 us
    all_gather x4, waiting for transfers between devices, body(): whole_rows = lax.all_gather(hstate, 'tp', axis=1, tiled=True)  74.5 us
    psum x4, blocking collectives, body(): rank_low = lax.psum(partial_low, 'tp').astype(jnp.bfloat16)  64.5 us
    all_to_all x2, blocking collectives, body(): lax.all_to_all(outgoing, 'req', split_axis=0, concat_axis=0, tiled=True)  46.1 us
    ppermute x3, waiting for transfers between devices, passed_along(): return lax.ppermute(block, axis, route)  37.6 us
    all_to_all x2, waiting for transfers between devices, body(): lax.all_to_all(outgoing, 'req', split_axis=0, concat_axis=0, tiled=True)  36.5 us
    unnamed x1, blocking collectives  33.5 us
    unnamed x97, local copies, waits for them, and re-layouts  24.3 us
  transfers between devices with their start and end apart: 12, of which 8 were waited for; matrix products, arithmetic and copies ran while one was open for 14% of the time, Pallas kernels for 0%

commit v1 on v0

--- a/solution.py
+++ b/solution.py
@@ -1,8 +1,11 @@
+import functools
 import math
 
 import jax
 import jax.numpy as jnp
 from jax import lax
+from jax.experimental import pallas as pl
+from jax.experimental.pallas import tpu as pltpu
 from jax.sharding import PartitionSpec as P
 
 D = 8192
@@ -22,6 +25,51 @@
     devices = range(lax.axis_size(axis))
     route = [(i - distance, i) for i in devices if i - distance in devices]
     return lax.ppermute(block, axis, route)
+
+
+def exchange_kernel(axis, n, gather, x_ref, o_ref, send_sem, recv_sem, local_sem):
+    me = lax.axis_index(axis)
+    barrier = pltpu.get_barrier_semaphore()
+    for j in range(1, n):
+        pl.semaphore_signal(
+            barrier, 1, device_id={axis: (me + j) % n}, device_id_type=pl.DeviceIdType.MESH
+        )
+    pl.semaphore_wait(barrier, n - 1)
+    copies = []
+    for j in range(1, n):
+        peer = (me + j) % n
+        copy = pltpu.make_async_remote_copy(
+            src_ref=x_ref if gather else x_ref.at[peer],
+            dst_ref=o_ref.at[me],
+            send_sem=send_sem.at[j],
+            recv_sem=recv_sem.at[j],
+            device_id={axis: peer},
+            device_id_type=pl.DeviceIdType.MESH,
+        )
+        copy.start()
+        copies.append(copy)
+    local = pltpu.make_async_copy(x_ref if gather else x_ref.at[me], o_ref.at[me], local_sem)
+    local.start()
+    local.wait()
+    for copy in copies:
+        copy.wait()
+
+
+def exchange(x, axis, collective_id, gather=False):
+    n = lax.axis_size(axis)
+    out_shape = (n,) + x.shape if gather else x.shape
+    return pl.pallas_call(
+        functools.partial(exchange_kernel, axis, n, gather),
+        out_shape=jax.ShapeDtypeStruct(out_shape, x.dtype),
+        in_specs=[pl.BlockSpec(memory_space=pl.ANY)],
+        out_specs=pl.BlockSpec(memory_space=pl.ANY),
+        scratch_shapes=[
+            pltpu.SemaphoreType.DMA((n,)),
+            pltpu.SemaphoreType.DMA((n,)),
+            pltpu.SemaphoreType.DMA(()),
+        ],
+        compiler_params=pltpu.CompilerParams(collective_id=collective_id, has_side_effects=True),
+    )(x)
 
 
 def rotate(key_vecs, positions):
@@ -93,6 +141,8 @@
     key_pos = jnp.arange(CTX, dtype=jnp.int32)
     causal = token_ids[None, :] <= token_ids[:, None]
     adapter_slots = jnp.arange(ADP_DEV, dtype=jnp.int32)
+    picks_out = jnp.zeros((req_count, batch_cap), jnp.int32).at[dest_all, slot_all].set(pick_all)
+    picks_in = lax.all_to_all(picks_out, "req", split_axis=0, concat_axis=0, tiled=True)
     carried = jnp.zeros((rows_per, width_loc), jnp.bfloat16)
     section_rows = jnp.zeros((RQ * S, width_loc), jnp.bfloat16)
     fresh_rows = jnp.zeros((RQ * S, 2, kv_width), jnp.bfloat16)
@@ -149,11 +199,7 @@
             .at[dest_all, slot_all]
             .set(attended)
         )
-        picks_out = (
-            jnp.zeros((req_count, batch_cap), jnp.int32).at[dest_all, slot_all].set(pick_all)
-        )
-        rows_in = lax.all_to_all(outgoing, "req", split_axis=0, concat_axis=0, tiled=True)
-        picks_in = lax.all_to_all(picks_out, "req", split_axis=0, concat_axis=0, tiled=True)
+        rows_in = exchange(outgoing, "req", 0)
         sources = rows_in.shape[0]
         item_count = rows_in.shape[1]
         flat_rows = rows_in.reshape(sources * item_count * S, q_width)
@@ -165,7 +211,7 @@
         )
         one_hot = (picks_rows[:, None] == adapter_slots[None, :]).astype(jnp.float32)
         partial_low = jnp.sum(all_low * one_hot[:, :, None], axis=1)
-        rank_low = lax.psum(partial_low, "tp").astype(jnp.bfloat16)
+        rank_low = jnp.sum(exchange(partial_low, "tp", 1, gather=True), axis=0).astype(jnp.bfloat16)
         spread = (rank_low.astype(jnp.float32)[:, None, :] * one_hot[:, :, None]).astype(
             jnp.bfloat16
         )
@@ -175,7 +221,7 @@
             preferred_element_type=jnp.float32,
         ).astype(jnp.bfloat16)
         deltas = deltas.reshape(sources, item_count, S, width_loc)
-        returned = lax.all_to_all(deltas, "req", split_axis=0, concat_axis=0, tiled=True)
+        returned = exchange(deltas, "req", 2)
         delta_rows = returned[dest_all, slot_all].reshape(rows_per, width_loc)
         new_state = (hstate.astype(jnp.float32) + delta_rows.astype(jnp.float32)).astype(
             jnp.bfloat16

time: 690 us -> 657 us (0.952)
  the two profiles are of different devices: /device:TPU:8 before, /device:TPU:89 now
where the time goes in v1:
time: 657 us; the launch traced here: 645 us
  Pallas kernels  244 us (37%)
  local copies, waits for them, and re-layouts  150 us (23%)
  waiting for transfers between devices  132 us (20%)
  matrix products  50.8 us (8%)
  other arithmetic  27.7 us (4%)
  between operations  16.3 us (2%)
  starting transfers between devices  13.2 us (2%)
  blocking collectives  11.1 us (2%)
    pallas_call x12, Pallas kernels, exchange(): pl.pallas_call(functools.partial(exchange_kernel, axis, n, gather), out_s...  244 us
    all_gather x4, waiting for transfers between devices, body(): whole_rows = lax.all_gather(hstate, 'tp', axis=1, tiled=True)  89.2 us
    ppermute x3, waiting for transfers between devices, passed_along(): return lax.ppermute(block, axis, route)  43 us
    unnamed x109, local copies, waits for them, and re-layouts  27 us
    scatter x1, local copies, waits for them, and re-layouts, body(): arrived = empty_pages.at[target].set(received, mode='drop')  24 us
    gather x2, local copies, waits for them, and re-layouts, body(): gathered = layer_pages[page_table]  17.7 us
    dot_general x4, matrix products, body(): jnp.dot(normed, weight_flat, preferred_element_type=jnp.float32)  16.6 us
    scatter x1, local copies, waits for them, and re-layouts, body(): written = layer_pages.at[page_slot, :, positions % PAGE, :].set(fresh_rows)  15.6 us
  transfers between devices with their start and end apart: 9, of which 6 were waited for; matrix products, arithmetic and copies ran while one was open for 11% of the time, Pallas kernels for 10%

profile of v1, /device:TPU:89, one launch (start us, length us, event | category | flops | bytes accessed | tf_op | source)
XLA Modules:
  0.0 644.7 jit_solution(363339042226429983)
XLA Ops:
  13.1 8.4 %all-to-all-start = ((s32[16,1,4]{2,1,0:T(1,128)}), s32[16,1,4]{2,1,0:T(1,128)S(1)}, u32[]{:S(2)}, u32[]{:S(2)}) async-start(s32[16,1,4]{2,1,0:T(1,128)} %copy.126), calls=%async_computation | async-start | bytes 16384 | tf_op jit(solution)/shard_map/all_to_all | solution.py:145
  22.6 12.8 %copy.165 = bf16[1,128,2,64,128]{4,2,3,1,0:T(2,128)(2,1)} copy(bf16[1,128,2,64,128]{4,3,2,1,0:T(8,128)(2,1)} %param.18) | data formatting | bytes 8388608 | tf_op args[6]
  35.6 14.2 %gather_fusion.1 = bf16[128,2,64,128]{3,1,2,0:T(2,128)(2,1)} fusion(bf16[128,2,64,128]{3,1,2,0:T(2,128)(2,1)} %bitcast.354, s32[1024]{0:T(1024)S(1)} %pad_clamp_fusion.1), kind=kCustom, calls=%fused_computation.1 | custom fusion | bytes 8389120 | tf_op jit(solution)/shard_map/gather | solution.py:165
  80.0 18.5 %shard_map.139 = bf16[16,4,4,1024]{3,2,1,0:T(4,128)(2,1)} custom-call(bf16[16,4,4,1024]{3,2,1,0:T(4,128)(2,1)} %copy-done.10), custom_call_target="tpu_custom_call" | custom-call | tf_op jit(solution)/shard_map/pallas_call | solution.py:61
  101.8 10.2 %shard_map.140 = f32[4,256,64]{2,1,0:T(8,128)} custom-call(f32[256,64]{1,0:T(8,128)} %copy.129.x_ref), custom_call_target="tpu_custom_call" | custom-call | tf_op jit(solution)/shard_map/pallas_call | solution.py:61
  117.2 30.8 %shard_map.141 = bf16[16,4,4,2048]{3,2,1,0:T(4,128)(2,1)} custom-call(bf16[16,4,4,2048]{3,2,1,0:T(4,128)(2,1)} %reshape.1474.x_ref), custom_call_target="tpu_custom_call" | custom-call | tf_op jit(solution)/shard_map/pallas_call | solution.py:61
  154.9 14.3 %collective-permute-done = bf16[128,2048]{1,0:T(8,128)(2,1)S(1)} collective-permute-done((bf16[128,2048]{1,0:T(8,128)(2,1)S(1)}, bf16[128,2048]{1,0:T(8,128)(2,1)S(1)}, u32[]{:S(2)}, u32[]{:S(2)}) %collective-permute-start) | collective-permute-done | bytes 524320 | tf_op jit(solution)/shard_map/ppermute | solution.py:27
  170.1 31.0 %all-gather.11.cloned.1.call-done = bf16[128,8192]{1,0:T(8,128)(2,1)} async-done(((bf16[128,2048]{1,0:T(8,128)(2,1)}), bf16[128,8192]{1,0:T(8,128)(2,1)}) %all-gather.11.cloned.1.call-update) | async-done | bytes 2097168 | tf_op jit(solution)/shard_map/all_gather | solution.py:153
  218.9 19.0 %shard_map.142 = bf16[16,4,4,1024]{3,2,1,0:T(4,128)(2,1)} custom-call(bf16[16,4,4,1024]{3,2,1,0:T(4,128)(2,1)} %copy-done.11), custom_call_target="tpu_custom_call" | custom-call | tf_op jit(solution)/shard_map/pallas_call | solution.py:61
  241.1 9.4 %shard_map.143 = f32[4,256,64]{2,1,0:T(8,128)} custom-call(f32[256,64]{1,0:T(8,128)} %copy.134.x_ref), custom_call_target="tpu_custom_call" | custom-call | tf_op jit(solution)/shard_map/pallas_call | solution.py:61
  255.6 30.5 %shard_map.144 = bf16[16,4,4,2048]{3,2,1,0:T(4,128)(2,1)} custom-call(bf16[16,4,4,2048]{3,2,1,0:T(4,128)(2,1)} %reshape.1478.x_ref), custom_call_target="tpu_custom_call" | custom-call | tf_op jit(solution)/shard_map/pallas_call | solution.py:61
  294.8 14.3 %collective-permute-done.1 = bf16[128,2048]{1,0:T(8,128)(2,1)S(1)} collective-permute-done((bf16[128,2048]{1,0:T(8,128)(2,1)S(1)}, bf16[128,2048]{1,0:T(8,128)(2,1)S(1)}, u32[]{:S(2)}, u32[]{:S(2)}) %collective-permute-start.1) | collective-permute-done | bytes 524320 | tf_op jit(solution)/shard_map/ppermute | solution.py:27
  310.3 31.0 %all-gather.13.cloned.1.call-done = bf16[128,8192]{1,0:T(8,128)(2,1)} async-done(((bf16[128,2048]{1,0:T(8,128)(2,1)}), bf16[128,8192]{1,0:T(8,128)(2,1)}) %all-gather.13.cloned.1.call-update) | async-done | bytes 2097168 | tf_op jit(solution)/shard_map/all_gather | solution.py:153
  360.2 19.0 %shard_map.145 = bf16[16,4,4,1024]{3,2,1,0:T(4,128)(2,1)} custom-call(bf16[16,4,4,1024]{3,2,1,0:T(4,128)(2,1)} %copy-done.12), custom_call_target="tpu_custom_call" | custom-call | tf_op jit(solution)/shard_map/pallas_call | solution.py:61
  382.5 9.4 %shard_map.146 = f32[4,256,64]{2,1,0:T(8,128)} custom-call(f32[256,64]{1,0:T(8,128)} %copy.139.x_ref), custom_call_target="tpu_custom_call" | custom-call | tf_op jit(solution)/shard_map/pallas_call | solution.py:61
  396.9 30.5 %shard_map.147 = bf16[16,4,4,2048]{3,2,1,0:T(4,128)(2,1)} custom-call(bf16[16,4,4,2048]{3,2,1,0:T(4,128)(2,1)} %reshape.1482.x_ref), custom_call_target="tpu_custom_call" | custom-call | tf_op jit(solution)/shard_map/pallas_call | solution.py:61
  436.1 14.3 %collective-permute-done.2 = bf16[128,2048]{1,0:T(8,128)(2,1)S(1)} collective-permute-done((bf16[128,2048]{1,0:T(8,128)(2,1)S(1)}, bf16[128,2048]{1,0:T(8,128)(2,1)S(1)}, u32[]{:S(2)}, u32[]{:S(2)}) %collective-permute-start.2) | collective-permute-done | bytes 524320 | tf_op jit(solution)/shard_map/ppermute | solution.py:27
  455.4 27.3 %all-gather.15.cloned.1.call-done = bf16[128,8192]{1,0:T(8,128)(2,1)} async-done(((bf16[128,2048]{1,0:T(8,128)(2,1)}), bf16[128,8192]{1,0:T(8,128)(2,1)}) %all-gather.15.cloned.1.call-update) | async-done | bytes 2097168 | tf_op jit(solution)/shard_map/all_gather | solution.py:153
  489.8 15.6 %scatter_fusion.5 = bf16[128,2,64,128]{3,1,2,0:T(2,128)(2,1)} fusion(bf16[128,2,64,128]{3,1,2,0:T(2,128)(2,1)} %bitcast.355, s32[128]{0:T(128)S(1)} %fusion.154, bf16[128,2,128]{2,1,0:T(2,128)(2,1)S(1)} %copy.146), kind=kCustom, calls=%fused_computation.13 | custom fusion | bytes 197632 | tf_op jit(solution)/shard_map/scatter | solution.py:235
  513.8 11.1 %all-reduce.2 = (s32[256]{0:T(256)S(1)}, s32[256]{0:T(256)S(1)}) all-reduce(s32[256]{0:T(256)S(1)} %bitcast_dynamic-update-slice_fusion, s32[256]{0:T(256)S(1)} %bitcast_dynamic-update-slice_fusion.1), channel_id=3, replica_groups=mesh['pipe'=4,'req'=16,'tp'=4] {'req'}, use_global_device_ids=true, to_apply=%add.1 | all-reduce | flops 512 | bytes 4096
  536.0 27.3 %shard_map.148 = bf16[16,4,4,1024]{3,2,1,0:T(4,128)(2,1)} custom-call(bf16[16,4,4,1024]{3,2,1,0:T(4,128)(2,1)} %copy-done.9), custom_call_target="tpu_custom_call" | custom-call | tf_op jit(solution)/shard_map/pallas_call | solution.py:61
  565.6 9.4 %shard_map.149 = f32[4,256,64]{2,1,0:T(8,128)} custom-call(f32[256,64]{1,0:T(8,128)} %copy.144.x_ref), custom_call_target="tpu_custom_call" | custom-call | tf_op jit(solution)/shard_map/pallas_call | solution.py:61
  578.0 29.6 %shard_map.150 = bf16[16,4,4,2048]{3,2,1,0:T(4,128)(2,1)} custom-call(bf16[16,4,4,2048]{3,2,1,0:T(4,128)(2,1)} %reshape.1486.x_ref), custom_call_target="tpu_custom_call" | custom-call | tf_op jit(solution)/shard_map/pallas_call | solution.py:61
  613.1 24.0 %scatter_fusion.6 = bf16[30,2,64,128]{3,2,1,0:T(8,128)(2,1)S(1)} fusion(bf16[30,2,64,128]{3,2,1,0:T(8,128)(2,1)S(1)} %broadcast_in_dim.93, s32[256]{0:T(256)S(1)} %compare_select_fusion.2, bf16[256,2,64,128]{3,2,1,0:T(8,128)(2,1)} %all-gather.17.cloned.1.call-done), kind=kCustom, calls=%fused_computation.14 | custom fusion | bytes 25166848 | tf_op jit(solution)/shard_map/scatter | solution.py:244
  (308 shorter events, 166.4 us)
Async XLA Ops:
  7.2 106.1 %copy-start = (bf16[1,4,64,2048]{3,2,1,0:T(8,128)(2,1)S(1)}, bf16[1,4,64,2048]{3,2,1,0:T(8,128)(2,1)}, u32[]{:S(2)}) copy-start(bf16[1,4,64,2048]{3,2,1,0:T(8,128)(2,1)} %param.17) | copy-start | bytes 3145732
  7.2 56.6 %all-gather.9.cloned.1.call-start = ((), (), s32[]{:S(2)}) async-start(), calls=%async_computation.1 | async-start | bytes 2621440 | tf_op jit(solution)/shard_map/all_gather | solution.py:153
  13.1 50.5 %all-to-all-start = ((s32[16,1,4]{2,1,0:T(1,128)}), s32[16,1,4]{2,1,0:T(1,128)S(1)}, u32[]{:S(2)}, u32[]{:S(2)}) async-start(s32[16,1,4]{2,1,0:T(1,128)} %copy.126), calls=%async_computation | async-start | bytes 16384 | tf_op jit(solution)/shard_map/all_to_all | solution.py:145
  21.5 179.6 %all-gather.11.cloned.1.call-start = ((), (), s32[]{:S(2)}) async-start(), calls=%async_computation.2 | async-start | bytes 2621440 | tf_op jit(solution)/shard_map/all_gather | solution.py:153
  22.6 48.0 %copy-start.21 = (bf16[16,8,8,128]{3,2,1,0:T(8,128)(2,1)}, bf16[16,8,8,128]{3,2,1,0:T(8,128)(2,1)S(1)}, u32[]{:S(2)}) copy-start(bf16[16,8,8,128]{3,2,1,0:T(8,128)(2,1)S(1)} %copy.160) | copy-start | bytes 786436
  53.4 16.7 %copy-start.41 = (f32[64]{0:T(128)}, f32[64]{0:T(128)S(1)}, u32[]{:S(2)}) copy-start(f32[64]{0:T(128)S(1)} %multiply_exponential_fusion) | copy-start | bytes 772
  53.4 17.2 %copy-start.48 = (pred[4,4]{1,0:T(4,128)(4,1)}, pred[4,4]{1,0:T(4,128)(4,1)S(1)}, u32[]{:S(2)}) copy-start(pred[4,4]{1,0:T(4,128)(4,1)S(1)} %iota_compare_fusion.3) | copy-start | bytes 52
  113.2 38.2 %copy-start.3 = (bf16[128,2048]{1,0:T(8,128)(2,1)S(1)}, bf16[128,2048]{1,0:T(8,128)(2,1)}, u32[]{:S(2)}) copy-start(bf16[128,2048]{1,0:T(8,128)(2,1)} %param.12) | copy-start | bytes 1572868
  150.3 52.9 %copy-start.34 = (f32[1,8192]{1,0:T(1,128)S(1)}, f32[1,8192]{1,0:T(1,128)}, u32[]{:S(2)}) copy-start(f32[1,8192]{1,0:T(1,128)} %copy-done.33) | copy-start | bytes 98308
  153.6 15.6 %collective-permute-start = (bf16[128,2048]{1,0:T(8,128)(2,1)S(1)}, bf16[128,2048]{1,0:T(8,128)(2,1)S(1)}, u32[]{:S(2)}, u32[]{:S(2)}) collective-permute-start(bf16[128,2048]{1,0:T(8,128)(2,1)S(1)} %add_convert_fusion.3), channel_id=1, source_target_pairs={{0,64},{64,128},{128,192},{1,65},{65,129},{129,193},{2,66},{66,130... | collective-permute-start | bytes 1572872 | tf_op jit(solution)/shard_map/ppermute | solution.py:27
  170.1 171.2 %all-gather.13.cloned.1.call-start = ((), (), s32[]{:S(2)}) async-start(), calls=%async_computation.3 | async-start | bytes 2621440 | tf_op jit(solution)/shard_map/all_gather | solution.py:153
  251.8 39.5 %copy-start.5 = (bf16[128,2048]{1,0:T(8,128)(2,1)S(1)}, bf16[128,2048]{1,0:T(8,128)(2,1)}, u32[]{:S(2)}) copy-start(bf16[128,2048]{1,0:T(8,128)(2,1)} %broadcast_select_fusion.2) | copy-start | bytes 1572868
  289.1 54.2 %copy-start.35 = (f32[1,8192]{1,0:T(1,128)S(1)}, f32[1,8192]{1,0:T(1,128)}, u32[]{:S(2)}) copy-start(f32[1,8192]{1,0:T(1,128)} %copy-done.33) | copy-start | bytes 98308
  293.5 15.6 %collective-permute-start.1 = (bf16[128,2048]{1,0:T(8,128)(2,1)S(1)}, bf16[128,2048]{1,0:T(8,128)(2,1)S(1)}, u32[]{:S(2)}, u32[]{:S(2)}) collective-permute-start(bf16[128,2048]{1,0:T(8,128)(2,1)S(1)} %add_convert_fusion.2), channel_id=1, source_target_pairs={{0,64},{64,128},{128,192},{1,65},{65,129},{129,193},{2,66},{66,130... | collective-permute-start | bytes 1572872 | tf_op jit(solution)/shard_map/ppermute | solution.py:27
  310.0 172.7 %all-gather.15.cloned.1.call-start = ((), (), s32[]{:S(2)}) async-start(), calls=%async_computation.4 | async-start | bytes 2621440 | tf_op jit(solution)/shard_map/all_gather | solution.py:153
  393.2 39.5 %copy-start.6 = (bf16[128,2048]{1,0:T(8,128)(2,1)S(1)}, bf16[128,2048]{1,0:T(8,128)(2,1)}, u32[]{:S(2)}) copy-start(bf16[128,2048]{1,0:T(8,128)(2,1)} %broadcast_select_fusion.1) | copy-start | bytes 1572868
  396.9 54.9 %copy-start.46 = (s32[32]{0:T(128)S(1)}, s32[32]{0:T(128)}, u32[]{:S(2)}) copy-start(s32[32]{0:T(128)} %param.22) | copy-start | bytes 388
  434.8 15.6 %collective-permute-start.2 = (bf16[128,2048]{1,0:T(8,128)(2,1)S(1)}, bf16[128,2048]{1,0:T(8,128)(2,1)S(1)}, u32[]{:S(2)}, u32[]{:S(2)}) collective-permute-start(bf16[128,2048]{1,0:T(8,128)(2,1)S(1)} %add_convert_fusion.1), channel_id=1, source_target_pairs={{0,64},{64,128},{128,192},{1,65},{65,129},{129,193},{2,66},{66,130... | collective-permute-start | bytes 1572872 | tf_op jit(solution)/shard_map/ppermute | solution.py:27
  451.3 161.6 %all-gather.17.cloned.1.call-start = ((), (), s32[]{:S(2)}) async-start(), calls=%async_computation.5 | async-start | bytes 8912896 | tf_op jit(solution)/shard_map/all_gather | solution.py:239
  452.0 32.7 %copy-start.36 = (f32[1,8192]{1,0:T(1,128)S(1)}, f32[1,8192]{1,0:T(1,128)}, u32[]{:S(2)}) copy-start(f32[1,8192]{1,0:T(1,128)} %copy-done.33) | copy-start | bytes 98308
  488.9 38.7 %copy-start.23 = (bf16[16,8,8,128]{3,2,1,0:T(8,128)(2,1)S(1)}, bf16[16,8,8,128]{3,2,1,0:T(8,128)(2,1)}, u32[]{:S(2)}) copy-start(bf16[16,8,8,128]{3,2,1,0:T(8,128)(2,1)} %copy-done.21) | copy-start | bytes 786436
  532.7 31.8 %copy-start.47 = (bf16[1,4,64,1024]{3,2,1,0:T(8,128)(2,1)S(1)}, bf16[1,4,64,1024]{3,2,1,0:T(8,128)(2,1)}, u32[]{:S(2)}) copy-start(bf16[1,4,64,1024]{3,2,1,0:T(8,128)(2,1)} %param.16) | copy-start | bytes 1572868
  576.3 35.5 %copy-start.4 = (bf16[128,2048]{1,0:T(8,128)(2,1)S(1)}, bf16[128,2048]{1,0:T(8,128)(2,1)}, u32[]{:S(2)}) copy-start(bf16[128,2048]{1,0:T(8,128)(2,1)} %broadcast_select_fusion) | copy-start | bytes 1572868
  576.3 35.5 %copy-start.14 = (bf16[128,2048]{1,0:T(8,128)(2,1)S(1)}, bf16[128,2048]{1,0:T(8,128)(2,1)}, u32[]{:S(2)}) copy-start(bf16[128,2048]{1,0:T(8,128)(2,1)} %copy-done.13) | copy-start | bytes 1572868
  (35 other events, 141.4 us)
Sparse Core Ops, SparseCore 0:
  10.4 35.3 all-gather.8
  170.2 30.8 all-gather.10
  310.1 31.1 all-gather.12
  451.4 31.2 all-gather.14
  510.4 65.6 all-gather.16

commit v2 on v1

--- a/solution.py
+++ b/solution.py
@@ -21,13 +21,20 @@
 CTX = 256
 
 
-def passed_along(block, axis, distance):
-    devices = range(lax.axis_size(axis))
-    route = [(i - distance, i) for i in devices if i - distance in devices]
-    return lax.ppermute(block, axis, route)
-
-
-def exchange_kernel(axis, n, gather, x_ref, o_ref, send_sem, recv_sem, local_sem):
+def passed_along(block, axis, source):
+    return lax.ppermute(block, axis, [(source, source + 1)])
+
+
+def exchange_kernel(axis, n, gather, gate, x_ref, o_ref, send_sem, recv_sem, local_sem):
+    if gate is None:
+        exchange_body(axis, n, gather, x_ref, o_ref, send_sem, recv_sem, local_sem)
+    else:
+        pl.when(lax.axis_index("pipe") == gate)(
+            lambda: exchange_body(axis, n, gather, x_ref, o_ref, send_sem, recv_sem, local_sem)
+        )
+
+
+def exchange_body(axis, n, gather, x_ref, o_ref, send_sem, recv_sem, local_sem):
     me = lax.axis_index(axis)
     barrier = pltpu.get_barrier_semaphore()
     for j in range(1, n):
@@ -55,11 +62,11 @@
         copy.wait()
 
 
-def exchange(x, axis, collective_id, gather=False):
+def exchange(x, axis, collective_id, gather=False, gate=None):
     n = lax.axis_size(axis)
     out_shape = (n,) + x.shape if gather else x.shape
     return pl.pallas_call(
-        functools.partial(exchange_kernel, axis, n, gather),
+        functools.partial(exchange_kernel, axis, n, gather, gate),
         out_shape=jax.ShapeDtypeStruct(out_shape, x.dtype),
         in_specs=[pl.BlockSpec(memory_space=pl.ANY)],
         out_specs=pl.BlockSpec(memory_space=pl.ANY),
@@ -141,8 +148,37 @@
     key_pos = jnp.arange(CTX, dtype=jnp.int32)
     causal = token_ids[None, :] <= token_ids[:, None]
     adapter_slots = jnp.arange(ADP_DEV, dtype=jnp.int32)
+    move_ids = jnp.arange(MOVES, dtype=jnp.int32)
+    move_dest = moves[:, 0]
+    move_slot = jnp.sum(
+        (
+            (move_ids[None, :] < move_ids[:, None]) & (move_dest[None, :] == move_dest[:, None])
+        ).astype(jnp.int32),
+        axis=1,
+    )
     picks_out = jnp.zeros((req_count, batch_cap), jnp.int32).at[dest_all, slot_all].set(pick_all)
-    picks_in = lax.all_to_all(picks_out, "req", split_axis=0, concat_axis=0, tiled=True)
+    spots_out = jnp.full((req_count, pair_cap), -1, jnp.int32).at[move_dest, move_slot].set(moves[:, 2])
+    ints_in = lax.all_to_all(
+        jnp.concatenate([picks_out, spots_out], axis=1), "req", split_axis=0, concat_axis=0, tiled=True
+    )
+    picks_in = ints_in[:, :batch_cap]
+    spots_in = ints_in[:, batch_cap:].reshape(req_count * pair_cap)
+    spot_match = spots_in[None, :] == jnp.arange(free_slots, dtype=jnp.int32)[:, None]
+    has_page = jnp.any(spot_match, axis=1)
+    page_src = jnp.argmax(spot_match, axis=1)
+    out_pages = (
+        jnp.zeros((req_count, pair_cap, 2, PAGE, kv_width), jnp.bfloat16)
+        .at[move_dest, move_slot]
+        .set(layer_pages[moves[:, 1]])
+    )
+    page_slot = jnp.take_along_axis(page_table, (positions // PAGE).reshape(RQ, S), axis=1).reshape(
+        RQ * S
+    )
+    tok_move = jnp.argmax(page_slot[:, None] == moves[None, :, 1], axis=1)
+    tok_moved = jnp.any(page_slot[:, None] == moves[None, :, 1], axis=1)
+    tok_dest = jnp.where(tok_moved, move_dest[tok_move], req_count)
+    tok_slot = move_slot[tok_move]
+    arrived = jnp.zeros((free_slots, 2, PAGE, kv_width), jnp.bfloat16)
     carried = jnp.zeros((rows_per, width_loc), jnp.bfloat16)
     section_rows = jnp.zeros((RQ * S, width_loc), jnp.bfloat16)
     fresh_rows = jnp.zeros((RQ * S, 2, kv_width), jnp.bfloat16)
@@ -228,20 +264,18 @@
         )
         section_rows = jnp.where(active, new_state, section_rows)
         fresh_rows = jnp.where(active, fresh_kv, fresh_rows)
-        carried = passed_along(new_state, "pipe", 1)
-    page_slot = jnp.take_along_axis(page_table, (positions // PAGE).reshape(RQ, S), axis=1).reshape(
-        RQ * S
-    )
-    written = layer_pages.at[page_slot, :, positions % PAGE, :].set(fresh_rows)
-    leaving = written[moves[:, 1]]
-    empty_pages = jnp.zeros((free_slots, 2, PAGE, kv_width), jnp.bfloat16)
-    received, dest_in, spots_in = (
-        lax.all_gather(leaving, "req", axis=0, tiled=True),
-        lax.all_gather(moves[:, 0], "req", axis=0, tiled=True),
-        lax.all_gather(moves[:, 2], "req", axis=0, tiled=True),
-    )
-    target = jnp.where(dest_in == my_req, spots_in, free_slots)
-    arrived = empty_pages.at[target].set(received, mode="drop")
+        if tick_id + 1 < section_count:
+            carried = passed_along(new_state, "pipe", tick_id)
+        sent_pages = out_pages.at[tok_dest, tok_slot, :, positions % PAGE, :].set(
+            fresh_kv, mode="drop"
+        )
+        got_pages = exchange(sent_pages, "req", 3 + tick_id, gate=tick_id).reshape(
+            req_count * pair_cap, 2, PAGE, kv_width
+        )
+        landed = jnp.where(
+            has_page[:, None, None, None], got_pages[page_src], jnp.zeros((), jnp.bfloat16)
+        )
+        arrived = jnp.where(section_id == tick_id, landed, arrived)
     return (section_rows[None], fresh_rows[None], arrived[None])
 
 

time: 657 us -> 678 us (1.032)
  waiting for transfers between devices: 132 us -> 90.6 us
  other arithmetic: 27.7 us -> 58.8 us
  local copies, waits for them, and re-layouts: 150 us -> 175 us
  Pallas kernels: 244 us -> 266 us
  blocking collectives: 11.1 us -> 0 us
    ppermute x3, waiting for transfers between devices: 43 us -> 12.6 us  [passed_along(): return lax.ppermute(block, axis, [(source, source + 1)])]
    pallas_call x12 -> x16, Pallas kernels: 244 us -> 266 us  [exchange(): pl.pallas_call(functools.partial(exchange_kernel, axis, n, gather, gate),...]
    concatenate x1, other arithmetic: 0.02 us -> 19.9 us  [body(): out_pages.at[tok_dest, tok_slot, :, positions % PAGE, :]]
    scatter x2 -> x11, local copies, waits for them, and re-layouts: 39.6 us -> 57.1 us  [the longest x8 50.7 us: body(): out_pages.at[tok_dest, tok_slot, :, positions % PAGE, :]]
    unnamed x109 -> x140, local copies, waits for them, and re-layouts: 27 us -> 12.6 us
    all_gather x4, waiting for transfers between devices: 89.2 us -> 77.9 us  [body(): whole_rows = lax.all_gather(hstate, 'tp', axis=1, tiled=True)]
    unnamed x1 -> x0, blocking collectives: 11.1 us -> none
    gather x2 -> x7, local copies, waits for them, and re-layouts: 4.86 us -> 15.9 us  [the longest x4 11.6 us: body(): got_pages[page_src]]
  transfers between devices with their start and end apart: 9 -> 8, of which waited for: 6 -> 3; matrix products, arithmetic and copies ran while one was open for 11% -> 18% of each run, Pallas kernels for 10% -> 0%
where the time goes in v2:
time: 678 us; the launch traced here: 672 us
  Pallas kernels  266 us (39%)
  local copies, waits for them, and re-layouts  175 us (26%)
  waiting for transfers between devices  90.6 us (13%)
  other arithmetic  58.8 us (9%)
  matrix products  52.8 us (8%)
  between operations  15.9 us (2%)
  starting transfers between devices  11.9 us (2%)
    pallas_call x16, Pallas kernels, exchange(): pl.pallas_call(functools.partial(exchange_kernel, axis, n, gather, gate),...  266 us
    all_gather x4, waiting for transfers between devices, body(): whole_rows = lax.all_gather(hstate, 'tp', axis=1, tiled=True)  77.9 us
    scatter x8, local copies, waits for them, and re-layouts, body(): out_pages.at[tok_dest, tok_slot, :, positions % PAGE, :]  50.7 us
    concatenate x1, other arithmetic, body(): out_pages.at[tok_dest, tok_slot, :, positions % PAGE, :]  19.9 us
    dot_general x4, matrix products, body(): jnp.dot(normed, weight_flat, preferred_element_type=jnp.float32)  16.7 us
  transfers between devices with their start and end apart: 8, of which 3 were waited for; matrix products, arithmetic and copies ran while one was open for 18% of the time, Pallas kernels for 0%

profile of v2, /device:TPU:89, one launch (start us, length us, event | category | flops | bytes accessed | tf_op | source)
XLA Modules:
  0.0 671.6 jit_solution(10273832698314581400)
XLA Ops:
  16.7 8.4 %all-to-all-start = ((s32[16,1,6]{2,1,0:T(1,128)}), s32[16,1,6]{2,1,0:T(1,128)S(1)}, u32[]{:S(2)}, u32[]{:S(2)}) async-start(s32[16,1,6]{2,1,0:T(1,128)} %copy.162), calls=%async_computation | async-start | bytes 16384 | tf_op jit(solution)/shard_map/all_to_all | solution.py:161
  28.1 5.2 gather_fusion.1
  40.8 6.4 copy.157
  64.0 18.5 %shard_map.139 = bf16[16,4,4,1024]{3,2,1,0:T(4,128)(2,1)} custom-call(bf16[16,4,4,1024]{3,2,1,0:T(4,128)(2,1)} %copy-done.13), custom_call_target="tpu_custom_call" | custom-call | tf_op jit(solution)/shard_map/pallas_call | solution.py:68
  85.8 10.1 %shard_map.140 = f32[4,256,64]{2,1,0:T(8,128)} custom-call(f32[256,64]{1,0:T(8,128)} %copy.165.x_ref), custom_call_target="tpu_custom_call" | custom-call | tf_op jit(solution)/shard_map/pallas_call | solution.py:68
  100.9 30.6 %shard_map.141 = bf16[16,4,4,2048]{3,2,1,0:T(4,128)(2,1)} custom-call(bf16[16,4,4,2048]{3,2,1,0:T(4,128)(2,1)} %reshape.1508.x_ref), custom_call_target="tpu_custom_call" | custom-call | tf_op jit(solution)/shard_map/pallas_call | solution.py:68
  138.9 44.1 %all-gather.7.cloned.1.call-done = bf16[128,8192]{1,0:T(8,128)(2,1)} async-done(((bf16[128,2048]{1,0:T(8,128)(2,1)}), bf16[128,8192]{1,0:T(8,128)(2,1)}) %all-gather.7.cloned.1.call-update) | async-done | bytes 2097168 | tf_op jit(solution)/shard_map/all_gather | solution.py:189
  201.6 19.0 %shard_map.142 = bf16[16,4,4,1024]{3,2,1,0:T(4,128)(2,1)} custom-call(bf16[16,4,4,1024]{3,2,1,0:T(4,128)(2,1)} %copy-done.14), custom_call_target="tpu_custom_call" | custom-call | tf_op jit(solution)/shard_map/pallas_call | solution.py:68
  223.8 9.4 %shard_map.143 = f32[4,256,64]{2,1,0:T(8,128)} custom-call(f32[256,64]{1,0:T(8,128)} %copy.170.x_ref), custom_call_target="tpu_custom_call" | custom-call | tf_op jit(solution)/shard_map/pallas_call | solution.py:68
  238.3 30.5 %shard_map.144 = bf16[16,4,4,2048]{3,2,1,0:T(4,128)(2,1)} custom-call(bf16[16,4,4,2048]{3,2,1,0:T(4,128)(2,1)} %reshape.1512.x_ref), custom_call_target="tpu_custom_call" | custom-call | tf_op jit(solution)/shard_map/pallas_call | solution.py:68
  290.2 33.8 %all-gather.9.cloned.1.call-done = bf16[128,8192]{1,0:T(8,128)(2,1)} async-done(((bf16[128,2048]{1,0:T(8,128)(2,1)}), bf16[128,8192]{1,0:T(8,128)(2,1)}) %all-gather.9.cloned.1.call-update) | async-done | bytes 2097168 | tf_op jit(solution)/shard_map/all_gather | solution.py:189
  348.9 19.0 %shard_map.145 = bf16[16,4,4,1024]{3,2,1,0:T(4,128)(2,1)} custom-call(bf16[16,4,4,1024]{3,2,1,0:T(4,128)(2,1)} %scatter_fusion.4), custom_call_target="tpu_custom_call" | custom-call | tf_op jit(solution)/shard_map/pallas_call | solution.py:68
  372.2 9.4 %shard_map.146 = f32[4,256,64]{2,1,0:T(8,128)} custom-call(f32[256,64]{1,0:T(8,128)} %copy.175.x_ref), custom_call_target="tpu_custom_call" | custom-call | tf_op jit(solution)/shard_map/pallas_call | solution.py:68
  386.7 30.6 %shard_map.147 = bf16[16,4,4,2048]{3,2,1,0:T(4,128)(2,1)} custom-call(bf16[16,4,4,2048]{3,2,1,0:T(4,128)(2,1)} %reshape.1516.x_ref), custom_call_target="tpu_custom_call" | custom-call | tf_op jit(solution)/shard_map/pallas_call | solution.py:68
  428.0 12.6 %collective-permute-done.2 = bf16[128,2048]{1,0:T(8,128)(2,1)} collective-permute-done((bf16[128,2048]{1,0:T(8,128)(2,1)}, bf16[128,2048]{1,0:T(8,128)(2,1)}, u32[]{:S(2)}, u32[]{:S(2)}) %collective-permute-start.2) | collective-permute-done | bytes 524320 | tf_op jit(solution)/shard_map/ppermute | solution.py:25
  443.2 19.9 %fusion.165 = s32[128]{0:T(128)S(1)} fusion(s32[128,1]{0,1:T(1,128)S(1)} %add.432, pred[128]{0:T(512)(128)(4,1)S(1)} %compare_reduce_fusion.1, s32[128]{0:T(128)S(1)} %get-tuple-element.5, s32[]{:T(128)} %bitcast.127, s32[]{:T(128)} %bitcast.128, s32[]{:T(128)} %bitcast.129, s32[]{:T(128)} %bitcast.130, s32[]{:T(128)} %bitcast.131, s32[]{:T(128)} %bitcast.132, ...), kind=kLoop, calls=%fused_computation.373 | loop fusion | flops 10624 | bytes 1792 | tf_op jit(solution)/shard_map/concatenate | solution.py:269
  466.1 7.3 %scatter_fusion.10 = bf16[16,2,2,64,128]{4,2,3,1,0:T(2,128)(2,1)S(1)} fusion(bf16[16,2,2,64,128]{4,2,3,1,0:T(2,128)(2,1)S(1)} %copy.183, s32[128]{0:T(128)S(1)} %fusion.165, bf16[128,2,128]{2,1,0:T(2,128)(2,1)S(1)} %copy.193), kind=kCustom, calls=%fused_computation.22 | custom fusion | bytes 198144 | tf_op jit(solution)/shard_map/scatter | solution.py:269
  481.0 17.2 %scatter_fusion.9 = bf16[16,2,2,64,128]{4,2,3,1,0:T(2,128)(2,1)} fusion(bf16[16,2,2,64,128]{4,2,3,1,0:T(2,128)(2,1)} %copy.218, s32[128]{0:T(128)S(1)} %fusion.165, bf16[128,2,128]{2,1,0:T(2,128)(2,1)S(1)} %copy.190), kind=kCustom, calls=%fused_computation.21 | custom fusion | bytes 198144 | tf_op jit(solution)/shard_map/scatter | solution.py:269
  506.9 7.3 %scatter_fusion.8 = bf16[16,2,2,64,128]{4,2,3,1,0:T(2,128)(2,1)S(1)} fusion(bf16[16,2,2,64,128]{4,2,3,1,0:T(2,128)(2,1)S(1)} %copy-done.6, s32[128]{0:T(128)S(1)} %fusion.165, bf16[128,2,128]{2,1,0:T(2,128)(2,1)S(1)} %copy.187), kind=kCustom, calls=%fused_computation.20 | custom fusion | bytes 198144 | tf_op jit(solution)/shard_map/scatter | solution.py:269
  533.7 12.6 %scatter_fusion.7 = bf16[16,2,2,64,128]{4,2,3,1,0:T(2,128)(2,1)S(1)} fusion(bf16[16,2,2,64,128]{4,2,3,1,0:T(2,128)(2,1)S(1)} %copy-done.5, s32[128]{0:T(128)S(1)} %fusion.165, bf16[128,2,128]{2,1,0:T(2,128)(2,1)} %copy.184), kind=kCustom, calls=%fused_computation.19 | custom fusion | bytes 198144 | tf_op jit(solution)/shard_map/scatter | solution.py:269
  547.6 30.1 %shard_map.151 = bf16[16,2,2,64,128]{4,3,2,1,0:T(8,128)(2,1)} custom-call(bf16[16,2,2,64,128]{4,3,2,1,0:T(8,128)(2,1)} %copy.185.x_ref), custom_call_target="tpu_custom_call" | custom-call | tf_op jit(solution)/shard_map/pallas_call | solution.py:68
  592.4 18.2 %shard_map.148 = bf16[16,4,4,1024]{3,2,1,0:T(4,128)(2,1)} custom-call(bf16[16,4,4,1024]{3,2,1,0:T(4,128)(2,1)} %copy-done.12), custom_call_target="tpu_custom_call" | custom-call | tf_op jit(solution)/shard_map/pallas_call | solution.py:68
  612.9 9.4 %shard_map.149 = f32[4,256,64]{2,1,0:T(8,128)} custom-call(f32[256,64]{1,0:T(8,128)} %copy.180.x_ref), custom_call_target="tpu_custom_call" | custom-call | tf_op jit(solution)/shard_map/pallas_call | solution.py:68
  625.3 30.6 %shard_map.150 = bf16[16,4,4,2048]{3,2,1,0:T(4,128)(2,1)} custom-call(bf16[16,4,4,2048]{3,2,1,0:T(4,128)(2,1)} %reshape.1520.x_ref), custom_call_target="tpu_custom_call" | custom-call | tf_op jit(solution)/shard_map/pallas_call | solution.py:68
  (376 shorter events, 215.4 us)
Async XLA Ops:
  7.2 90.0 %copy-start = (bf16[1,4,64,2048]{3,2,1,0:T(8,128)(2,1)S(1)}, bf16[1,4,64,2048]{3,2,1,0:T(8,128)(2,1)}, u32[]{:S(2)}) copy-start(bf16[1,4,64,2048]{3,2,1,0:T(8,128)(2,1)} %param.17) | copy-start | bytes 3145732
  7.2 40.5 %all-gather.5.cloned.1.call-start = ((), (), s32[]{:S(2)}) async-start(), calls=%async_computation.1 | async-start | bytes 2621440 | tf_op jit(solution)/shard_map/all_gather | solution.py:189
  16.7 30.6 %all-to-all-start = ((s32[16,1,6]{2,1,0:T(1,128)}), s32[16,1,6]{2,1,0:T(1,128)S(1)}, u32[]{:S(2)}, u32[]{:S(2)}) async-start(s32[16,1,6]{2,1,0:T(1,128)} %copy.162), calls=%async_computation | async-start | bytes 16384 | tf_op jit(solution)/shard_map/all_to_all | solution.py:161
  25.1 157.9 %all-gather.7.cloned.1.call-start = ((), (), s32[]{:S(2)}) async-start(), calls=%async_computation.2 | async-start | bytes 2621440 | tf_op jit(solution)/shard_map/all_gather | solution.py:189
  25.8 164.6 %copy-start.19 = (bf16[16,8,8,128]{3,2,1,0:T(8,128)(2,1)}, bf16[16,8,8,128]{3,2,1,0:T(8,128)(2,1)S(1)}, u32[]{:S(2)}) copy-start(bf16[16,8,8,128]{3,2,1,0:T(8,128)(2,1)S(1)} %copy.206) | copy-start | bytes 786436
  36.7 294.2 %copy-start.56 = (f32[64]{0:T(128)}, f32[64]{0:T(128)S(1)}, u32[]{:S(2)}) copy-start(f32[64]{0:T(128)S(1)} %multiply_exponential_fusion) | copy-start | bytes 772
  37.3 293.6 %copy-start.53 = (f32[128]{0:T(128)}, f32[128]{0:T(128)S(1)}, u32[]{:S(2)}) copy-start(f32[128]{0:T(128)S(1)} %get-tuple-element.69) | copy-start | bytes 1540
  38.3 152.1 %copy-start.65 = (pred[4,4]{1,0:T(4,128)(4,1)}, pred[4,4]{1,0:T(4,128)(4,1)S(1)}, u32[]{:S(2)}) copy-start(pred[4,4]{1,0:T(4,128)(4,1)S(1)} %iota_compare_fusion.5) | copy-start | bytes 52
  47.7 186.8 %copy-start.42 = (f32[256,4]{0,1:T(4,128)}, f32[256,4]{0,1:T(4,128)S(1)}, u32[]{:S(2)}) copy-start(f32[256,4]{0,1:T(4,128)S(1)} %fusion.154) | copy-start | bytes 12292
  133.8 51.3 %copy-start.51 = (f32[1,8192]{1,0:T(1,128)S(1)}, f32[1,8192]{1,0:T(1,128)}, u32[]{:S(2)}) copy-start(f32[1,8192]{1,0:T(1,128)} %copy-done.50) | copy-start | bytes 98308
  137.1 0.9 collective-permute-start
  138.8 185.2 %all-gather.9.cloned.1.call-start = ((), (), s32[]{:S(2)}) async-start(), calls=%async_computation.3 | async-start | bytes 2621440 | tf_op jit(solution)/shard_map/all_gather | solution.py:189
  276.2 0.7 collective-permute-start.1
  277.8 243.1 %all-gather.11.cloned.1.call-start = ((), (), s32[]{:S(2)}) async-start(), calls=%async_computation.4 | async-start | bytes 2621440 | tf_op jit(solution)/shard_map/all_gather | solution.py:189
  384.3 42.0 %copy-start.59 = (s32[32]{0:T(128)S(1)}, s32[32]{0:T(128)}, u32[]{:S(2)}) copy-start(s32[32]{0:T(128)} %param.22) | copy-start | bytes 388
  384.3 42.9 %copy-start.46 = (s32[16,3]{0,1:T(4,128)S(1)}, s32[16,3]{0,1:T(4,128)}, u32[]{:S(2)}) copy-start(s32[16,3]{0,1:T(4,128)} %param.23) | copy-start | bytes 580
  384.3 43.6 %copy-start.60 = (s32[128]{0:T(128)S(1)}, s32[128]{0:T(128)}, u32[]{:S(2)}) copy-start(s32[128]{0:T(128)} %get-tuple-element.68) | copy-start | bytes 1540
  384.3 43.6 %copy-start.62 = (s32[16]{0:T(128)S(1)}, s32[16]{0:T(128)}, u32[]{:S(2)}) copy-start(s32[16]{0:T(128)} %get-tuple-element.46) | copy-start | bytes 196
  386.7 79.3 %copy-start.22 = (bf16[128,1,64]{0,2,1:T(8,128)(2,1)S(1)}, bf16[128,1,64]{0,2,1:T(8,128)(2,1)}, u32[]{:S(2)}) copy-start(bf16[128,1,64]{0,2,1:T(8,128)(2,1)} %copy-done.21) | copy-start | bytes 49156
  386.7 79.3 %copy-start.24 = (bf16[128,1,64]{0,2,1:T(8,128)(2,1)S(1)}, bf16[128,1,64]{0,2,1:T(8,128)(2,1)}, u32[]{:S(2)}) copy-start(bf16[128,1,64]{0,2,1:T(8,128)(2,1)} %copy-done.23) | copy-start | bytes 49156
  424.7 15.9 %collective-permute-start.2 = (bf16[128,2048]{1,0:T(8,128)(2,1)}, bf16[128,2048]{1,0:T(8,128)(2,1)}, u32[]{:S(2)}, u32[]{:S(2)}) collective-permute-start(bf16[128,2048]{1,0:T(8,128)(2,1)} %add_convert_fusion.1), channel_id=1, source_target_pairs={{128,192},{129,193},{130,194},{131,195},{132,196},{133,197},{134,1... | collective-permute-start | bytes 1572872 | tf_op jit(solution)/shard_map/ppermute | solution.py:25
  527.2 55.0 %copy-start.20 = (bf16[16,8,8,128]{3,2,1,0:T(8,128)(2,1)S(1)}, bf16[16,8,8,128]{3,2,1,0:T(8,128)(2,1)}, u32[]{:S(2)}) copy-start(bf16[16,8,8,128]{3,2,1,0:T(8,128)(2,1)} %copy-done.19) | copy-start | bytes 786436
  533.7 46.9 %copy-start.39 = (bf16[1,128,1,128]{1,3,2,0:T(8,128)(2,1)S(1)}, bf16[1,128,1,128]{1,3,2,0:T(8,128)(2,1)}, u32[]{:S(2)}) copy-start(bf16[1,128,1,128]{1,3,2,0:T(8,128)(2,1)} %maximum_bitcast_fusion.11) | copy-start | bytes 98308
  533.7 46.9 %copy-start.40 = (bf16[1,128,1,128]{1,3,2,0:T(8,128)(2,1)S(1)}, bf16[1,128,1,128]{1,3,2,0:T(8,128)(2,1)}, u32[]{:S(2)}) copy-start(bf16[1,128,1,128]{1,3,2,0:T(8,128)(2,1)} %slice_bitcast_fusion.23) | copy-start | bytes 98308
  (51 other events, 704.7 us)
Sparse Core Ops, SparseCore 0:
  10.4 35.3 all-gather.4
  139.0 44.0 all-gather.6
  277.9 46.0 all-gather.8
  442.7 30.8 all-gather.10

commit v3 on v2

--- a/solution.py
+++ b/solution.py
@@ -166,19 +166,24 @@
     spot_match = spots_in[None, :] == jnp.arange(free_slots, dtype=jnp.int32)[:, None]
     has_page = jnp.any(spot_match, axis=1)
     page_src = jnp.argmax(spot_match, axis=1)
-    out_pages = (
-        jnp.zeros((req_count, pair_cap, 2, PAGE, kv_width), jnp.bfloat16)
-        .at[move_dest, move_slot]
-        .set(layer_pages[moves[:, 1]])
+    box_ids = jnp.arange(req_count * pair_cap, dtype=jnp.int32)
+    box_match = (move_dest * pair_cap + move_slot)[None, :] == box_ids[:, None]
+    box_move = jnp.argmax(box_match, axis=1)
+    box_used = jnp.any(box_match, axis=1)
+    box_page = jnp.where(box_used, moves[box_move, 1], -1)
+    out_pages = jnp.where(
+        box_used[:, None, None, None], layer_pages[moves[box_move, 1]], jnp.zeros((), jnp.bfloat16)
     )
     page_slot = jnp.take_along_axis(page_table, (positions // PAGE).reshape(RQ, S), axis=1).reshape(
         RQ * S
     )
-    tok_move = jnp.argmax(page_slot[:, None] == moves[None, :, 1], axis=1)
-    tok_moved = jnp.any(page_slot[:, None] == moves[None, :, 1], axis=1)
-    tok_dest = jnp.where(tok_moved, move_dest[tok_move], req_count)
-    tok_slot = move_slot[tok_move]
-    arrived = jnp.zeros((free_slots, 2, PAGE, kv_width), jnp.bfloat16)
+    spot_ids = jnp.arange(req_count * pair_cap * PAGE, dtype=jnp.int32)
+    tok_match = (
+        (page_slot[None, :] == box_page[spot_ids // PAGE][:, None])
+        & ((positions % PAGE)[None, :] == (spot_ids % PAGE)[:, None])
+    )
+    tok_pick = tok_match.astype(jnp.bfloat16)
+    tok_hit = jnp.any(tok_match, axis=1).reshape(req_count * pair_cap, PAGE)
     carried = jnp.zeros((rows_per, width_loc), jnp.bfloat16)
     section_rows = jnp.zeros((RQ * S, width_loc), jnp.bfloat16)
     fresh_rows = jnp.zeros((RQ * S, 2, kv_width), jnp.bfloat16)
@@ -266,16 +271,18 @@
         fresh_rows = jnp.where(active, fresh_kv, fresh_rows)
         if tick_id + 1 < section_count:
             carried = passed_along(new_state, "pipe", tick_id)
-        sent_pages = out_pages.at[tok_dest, tok_slot, :, positions % PAGE, :].set(
-            fresh_kv, mode="drop"
-        )
-        got_pages = exchange(sent_pages, "req", 3 + tick_id, gate=tick_id).reshape(
-            req_count * pair_cap, 2, PAGE, kv_width
-        )
-        landed = jnp.where(
-            has_page[:, None, None, None], got_pages[page_src], jnp.zeros((), jnp.bfloat16)
-        )
-        arrived = jnp.where(section_id == tick_id, landed, arrived)
+
+    patch = jnp.dot(
+        tok_pick, fresh_rows.reshape(RQ * S, 2 * kv_width), preferred_element_type=jnp.float32
+    ).astype(jnp.bfloat16)
+    patch = jnp.swapaxes(patch.reshape(req_count * pair_cap, PAGE, 2, kv_width), 1, 2)
+    sent_pages = jnp.where(tok_hit[:, None, :, None], patch, out_pages).reshape(
+        req_count, pair_cap, 2, PAGE, kv_width
+    )
+    got_pages = exchange(sent_pages, "req", 3).reshape(req_count * pair_cap, 2, PAGE, kv_width)
+    arrived = jnp.where(
+        has_page[:, None, None, None], got_pages[page_src], jnp.zeros((), jnp.bfloat16)
+    )
     return (section_rows[None], fresh_rows[None], arrived[None])
 
 

time: 678 us -> 606 us (0.89)
  local copies, waits for them, and re-layouts: 175 us -> 96.2 us
  other arithmetic: 58.8 us -> 72.3 us
    scatter x10 -> x0, local copies, waits for them, and re-layouts: 55.8 us -> none  [the longest x8 50.7 us: body(): out_pages.at[tok_dest, tok_slot, :, positions % PAGE, :]]
    gather x1 -> x28, other arithmetic: 0.01 us -> 32.4 us  [the longest x27 32.4 us: body(): box_page[spot_ids // PAGE][:, None]]
    concatenate x1, other arithmetic: 19.9 us -> 0.01 us  [body(): box_page = jnp.where(box_used, moves[box_move, 1], -1)]
    gather x4 -> x1, local copies, waits for them, and re-layouts: 11.6 us -> 2.08 us  [body(): got_pages[page_src]]
    ppermute x3, waiting for transfers between devices: 12.6 us -> 4.03 us  [passed_along(): return lax.ppermute(block, axis, [(source, source + 1)])]
    pallas_call x16 -> x13, Pallas kernels: 266 us -> 265 us  [exchange(): pl.pallas_call(functools.partial(exchange_kernel, axis, n, gather, gate),...]
  transfers between devices with their start and end apart: 8 -> 8, of which waited for: 3 -> 3; matrix products, arithmetic and copies ran while one was open for 18% -> 14% of each run, Pallas kernels for 0% -> 0%
where the time goes in v3:
time: 606 us; the launch traced here: 601 us
  Pallas kernels  265 us (44%)
  local copies, waits for them, and re-layouts  96.2 us (16%)
  waiting for transfers between devices  84.9 us (14%)
  other arithmetic  72.3 us (12%)
  matrix products  54.2 us (9%)
  between operations  15.8 us (3%)
  starting transfers between devices  11.8 us (2%)
    pallas_call x13, Pallas kernels, exchange(): pl.pallas_call(functools.partial(exchange_kernel, axis, n, gather, gate),...  265 us
    all_gather x4, waiting for transfers between devices, body(): whole_rows = lax.all_gather(hstate, 'tp', axis=1, tiled=True)  80.8 us
    gather x27, other arithmetic, body(): box_page[spot_ids // PAGE][:, None]  32.4 us
    dot_general x4, matrix products, body(): jnp.dot(normed, weight_flat, preferred_element_type=jnp.float32)  16.7 us
  transfers between devices with their start and end apart: 8, of which 3 were waited for; matrix products, arithmetic and copies ran while one was open for 14% of the time, Pallas kernels for 0%

profile of v3, /device:TPU:89, one launch (start us, length us, event | category | flops | bytes accessed | tf_op | source)
XLA Modules:
  0.0 600.7 jit_solution(11716331302385565571)
XLA Ops:
  16.1 8.4 %all-to-all-start = ((s32[16,1,6]{2,1,0:T(1,128)}), s32[16,1,6]{2,1,0:T(1,128)S(1)}, u32[]{:S(2)}, u32[]{:S(2)}) async-start(s32[16,1,6]{2,1,0:T(1,128)} %copy.122), calls=%async_computation | async-start | bytes 16384 | tf_op jit(solution)/shard_map/all_to_all | solution.py:161
  27.3 5.2 gather_fusion.1
  40.1 6.4 %copy.117 = bf16[256,8192]{1,0:T(8,128)(2,1)} copy(bf16[256,8192]{0,1:T(8,128)(2,1)} %bitcast.393) | data formatting | bytes 8388608 | tf_op jit(solution)/shard_map/dot_general | solution.py:198
  49.6 4.2 fusion.22
  63.8 18.5 %shard_map.139 = bf16[16,4,4,1024]{3,2,1,0:T(4,128)(2,1)} custom-call(bf16[16,4,4,1024]{3,2,1,0:T(4,128)(2,1)} %copy-done.10), custom_call_target="tpu_custom_call" | custom-call | tf_op jit(solution)/shard_map/pallas_call | solution.py:68
  85.6 10.1 %shard_map.140 = f32[4,256,64]{2,1,0:T(8,128)} custom-call(f32[256,64]{1,0:T(8,128)} %copy.125.x_ref), custom_call_target="tpu_custom_call" | custom-call | tf_op jit(solution)/shard_map/pallas_call | solution.py:68
  100.7 30.5 %shard_map.141 = bf16[16,4,4,2048]{3,2,1,0:T(4,128)(2,1)} custom-call(bf16[16,4,4,2048]{3,2,1,0:T(4,128)(2,1)} %reshape.1486.x_ref), custom_call_target="tpu_custom_call" | custom-call | tf_op jit(solution)/shard_map/pallas_call | solution.py:68
  139.1 43.9 %all-gather.7.cloned.1.call-done = bf16[128,8192]{1,0:T(8,128)(2,1)} async-done(((bf16[128,2048]{1,0:T(8,128)(2,1)}), bf16[128,8192]{1,0:T(8,128)(2,1)}) %all-gather.7.cloned.1.call-update) | async-done | bytes 2097168 | tf_op jit(solution)/shard_map/all_gather | solution.py:194
  185.0 4.2 fusion.57
  199.3 19.0 %shard_map.142 = bf16[16,4,4,1024]{3,2,1,0:T(4,128)(2,1)} custom-call(bf16[16,4,4,1024]{3,2,1,0:T(4,128)(2,1)} %copy-done.11), custom_call_target="tpu_custom_call" | custom-call | tf_op jit(solution)/shard_map/pallas_call | solution.py:68
  221.6 9.4 %shard_map.143 = f32[4,256,64]{2,1,0:T(8,128)} custom-call(f32[256,64]{1,0:T(8,128)} %copy.130.x_ref), custom_call_target="tpu_custom_call" | custom-call | tf_op jit(solution)/shard_map/pallas_call | solution.py:68
  236.1 30.6 %shard_map.144 = bf16[16,4,4,2048]{3,2,1,0:T(4,128)(2,1)} custom-call(bf16[16,4,4,2048]{3,2,1,0:T(4,128)(2,1)} %reshape.1490.x_ref), custom_call_target="tpu_custom_call" | custom-call | tf_op jit(solution)/shard_map/pallas_call | solution.py:68
  284.9 37.0 %all-gather.9.cloned.1.call-done = bf16[128,8192]{1,0:T(8,128)(2,1)} async-done(((bf16[128,2048]{1,0:T(8,128)(2,1)}), bf16[128,8192]{1,0:T(8,128)(2,1)}) %all-gather.9.cloned.1.call-update) | async-done | bytes 2097168 | tf_op jit(solution)/shard_map/all_gather | solution.py:194
  324.0 4.2 fusion.60
  340.8 19.0 %shard_map.145 = bf16[16,4,4,1024]{3,2,1,0:T(4,128)(2,1)} custom-call(bf16[16,4,4,1024]{3,2,1,0:T(4,128)(2,1)} %copy-done.12), custom_call_target="tpu_custom_call" | custom-call | tf_op jit(solution)/shard_map/pallas_call | solution.py:68
  363.1 9.4 %shard_map.146 = f32[4,256,64]{2,1,0:T(8,128)} custom-call(f32[256,64]{1,0:T(8,128)} %copy.135.x_ref), custom_call_target="tpu_custom_call" | custom-call | tf_op jit(solution)/shard_map/pallas_call | solution.py:68
  377.6 30.8 %shard_map.147 = bf16[16,4,4,2048]{3,2,1,0:T(4,128)(2,1)} custom-call(bf16[16,4,4,2048]{3,2,1,0:T(4,128)(2,1)} %reshape.1494.x_ref), custom_call_target="tpu_custom_call" | custom-call | tf_op jit(solution)/shard_map/pallas_call | solution.py:68
  423.3 4.3 compare_select_fusion.2
  432.6 16.2 %select_select_fusion = s32[2048]{0:T(1024)S(1)} fusion(pred[2048]{0:T(1024)(128)(4,1)S(1)} %copy-done.53, pred[2048]{0:T(1024)(128)(4,1)S(1)} %copy-done.54, pred[2048]{0:T(1024)(128)(4,1)S(1)} %compare_reduce_fusion.2, pred[2048]{0:T(1024)(128)(4,1)} %compare_reduce_fusion.3, pred[2048]{0:T(1024)(128)(4,1)} %compare_reduce_fusion.4, ...), kind=kLoop, calls=%fused_computation.298 | loop fusion | flops 51200 | bytes 67684 | tf_op jit(solution)/shard_map/gather | solution.py:182
  467.1 4.2 fusion.63
  481.1 30.0 %shard_map.151 = bf16[16,2,2,64,128]{4,3,2,1,0:T(8,128)(2,1)} custom-call(bf16[16,2,2,64,128]{4,3,2,1,0:T(8,128)(2,1)} %bitcast.406), custom_call_target="tpu_custom_call" | custom-call | tf_op jit(solution)/shard_map/pallas_call | solution.py:68
  522.0 18.2 %shard_map.148 = bf16[16,4,4,1024]{3,2,1,0:T(4,128)(2,1)} custom-call(bf16[16,4,4,1024]{3,2,1,0:T(4,128)(2,1)} %copy-done.9), custom_call_target="tpu_custom_call" | custom-call | tf_op jit(solution)/shard_map/pallas_call | solution.py:68
  542.6 9.4 %shard_map.149 = f32[4,256,64]{2,1,0:T(8,128)} custom-call(f32[256,64]{1,0:T(8,128)} %copy.140.x_ref), custom_call_target="tpu_custom_call" | custom-call | tf_op jit(solution)/shard_map/pallas_call | solution.py:68
  555.0 30.5 %shard_map.150 = bf16[16,4,4,2048]{3,2,1,0:T(4,128)(2,1)} custom-call(bf16[16,4,4,2048]{3,2,1,0:T(4,128)(2,1)} %reshape.1498.x_ref), custom_call_target="tpu_custom_call" | custom-call | tf_op jit(solution)/shard_map/pallas_call | solution.py:68
  (400 shorter events, 181.4 us)
Async XLA Ops:
  7.2 89.8 %copy-start = (bf16[1,4,64,2048]{3,2,1,0:T(8,128)(2,1)S(1)}, bf16[1,4,64,2048]{3,2,1,0:T(8,128)(2,1)}, u32[]{:S(2)}) copy-start(bf16[1,4,64,2048]{3,2,1,0:T(8,128)(2,1)} %param.17) | copy-start | bytes 3145732
  7.2 40.3 %all-gather.5.cloned.1.call-start = ((), (), s32[]{:S(2)}) async-start(), calls=%async_computation.1 | async-start | bytes 2621440 | tf_op jit(solution)/shard_map/all_gather | solution.py:194
  16.1 30.5 %all-to-all-start = ((s32[16,1,6]{2,1,0:T(1,128)}), s32[16,1,6]{2,1,0:T(1,128)S(1)}, u32[]{:S(2)}, u32[]{:S(2)}) async-start(s32[16,1,6]{2,1,0:T(1,128)} %copy.122), calls=%async_computation | async-start | bytes 16384 | tf_op jit(solution)/shard_map/all_to_all | solution.py:161
  24.5 158.4 %all-gather.7.cloned.1.call-start = ((), (), s32[]{:S(2)}) async-start(), calls=%async_computation.2 | async-start | bytes 2621440 | tf_op jit(solution)/shard_map/all_gather | solution.py:194
  36.6 152.7 %copy-start.45 = (f32[128]{0:T(128)}, f32[128]{0:T(128)S(1)}, u32[]{:S(2)}) copy-start(f32[128]{0:T(128)S(1)} %get-tuple-element.33) | copy-start | bytes 1540
  133.6 51.5 %copy-start.43 = (f32[1,8192]{1,0:T(1,128)S(1)}, f32[1,8192]{1,0:T(1,128)}, u32[]{:S(2)}) copy-start(f32[1,8192]{1,0:T(1,128)} %copy-done.42) | copy-start | bytes 98308
  136.9 1.2 collective-permute-start
  139.0 182.9 %all-gather.9.cloned.1.call-start = ((), (), s32[]{:S(2)}) async-start(), calls=%async_computation.3 | async-start | bytes 2621440 | tf_op jit(solution)/shard_map/all_gather | solution.py:194
  269.7 54.3 %copy-start.44 = (f32[1,8192]{1,0:T(1,128)S(1)}, f32[1,8192]{1,0:T(1,128)}, u32[]{:S(2)}) copy-start(f32[1,8192]{1,0:T(1,128)} %copy-done.42) | copy-start | bytes 98308
  274.1 0.7 collective-permute-start.1
  275.6 189.3 %all-gather.11.cloned.1.call-start = ((), (), s32[]{:S(2)}) async-start(), calls=%async_computation.4 | async-start | bytes 2621440 | tf_op jit(solution)/shard_map/all_gather | solution.py:194
  377.5 55.0 %copy-start.53 = (pred[2048]{0:T(1024)(128)(4,1)S(1)}, pred[2048]{0:T(1024)(128)(4,1)}, u32[]{:S(2)}) copy-start(pred[2048]{0:T(1024)(128)(4,1)} %compare_reduce_fusion) | copy-start | bytes 6148
  377.5 55.0 %copy-start.54 = (pred[2048]{0:T(1024)(128)(4,1)S(1)}, pred[2048]{0:T(1024)(128)(4,1)}, u32[]{:S(2)}) copy-start(pred[2048]{0:T(1024)(128)(4,1)} %compare_reduce_fusion.1) | copy-start | bytes 6148
  377.5 55.0 %copy-start.55 = (pred[2048]{0:T(1024)(128)(4,1)S(1)}, pred[2048]{0:T(1024)(128)(4,1)}, u32[]{:S(2)}) copy-start(pred[2048]{0:T(1024)(128)(4,1)} %compare_reduce_fusion.10) | copy-start | bytes 6148
  377.5 55.0 %copy-start.56 = (pred[2048]{0:T(1024)(128)(4,1)S(1)}, pred[2048]{0:T(1024)(128)(4,1)}, u32[]{:S(2)}) copy-start(pred[2048]{0:T(1024)(128)(4,1)} %compare_reduce_fusion.11) | copy-start | bytes 6148
  377.5 55.0 %copy-start.57 = (pred[2048]{0:T(1024)(128)(4,1)S(1)}, pred[2048]{0:T(1024)(128)(4,1)}, u32[]{:S(2)}) copy-start(pred[2048]{0:T(1024)(128)(4,1)} %compare_reduce_fusion.12) | copy-start | bytes 6148
  377.5 55.0 %copy-start.58 = (pred[2048]{0:T(1024)(128)(4,1)S(1)}, pred[2048]{0:T(1024)(128)(4,1)}, u32[]{:S(2)}) copy-start(pred[2048]{0:T(1024)(128)(4,1)} %compare_reduce_fusion.13) | copy-start | bytes 6148
  377.6 55.0 %copy-start.59 = (pred[2048]{0:T(1024)(128)(4,1)S(1)}, pred[2048]{0:T(1024)(128)(4,1)}, u32[]{:S(2)}) copy-start(pred[2048]{0:T(1024)(128)(4,1)} %compare_reduce_fusion.14) | copy-start | bytes 6148
  377.6 55.0 %copy-start.60 = (pred[2048]{0:T(1024)(128)(4,1)S(1)}, pred[2048]{0:T(1024)(128)(4,1)}, u32[]{:S(2)}) copy-start(pred[2048]{0:T(1024)(128)(4,1)} %compare_reduce_fusion.15) | copy-start | bytes 6148
  377.6 55.0 %copy-start.61 = (pred[2048]{0:T(1024)(128)(4,1)S(1)}, pred[2048]{0:T(1024)(128)(4,1)}, u32[]{:S(2)}) copy-start(pred[2048]{0:T(1024)(128)(4,1)} %compare_reduce_fusion.16) | copy-start | bytes 6148
  377.6 55.0 %copy-start.62 = (pred[2048]{0:T(1024)(128)(4,1)S(1)}, pred[2048]{0:T(1024)(128)(4,1)}, u32[]{:S(2)}) copy-start(pred[2048]{0:T(1024)(128)(4,1)} %compare_reduce_fusion.17) | copy-start | bytes 6148
  377.6 55.0 %copy-start.63 = (pred[2048]{0:T(1024)(128)(4,1)S(1)}, pred[2048]{0:T(1024)(128)(4,1)}, u32[]{:S(2)}) copy-start(pred[2048]{0:T(1024)(128)(4,1)} %compare_reduce_fusion.18) | copy-start | bytes 6148
  377.6 55.0 %copy-start.64 = (pred[2048]{0:T(1024)(128)(4,1)S(1)}, pred[2048]{0:T(1024)(128)(4,1)}, u32[]{:S(2)}) copy-start(pred[2048]{0:T(1024)(128)(4,1)} %compare_reduce_fusion.19) | copy-start | bytes 6148
  415.8 15.8 %collective-permute-start.2 = (bf16[128,2048]{1,0:T(8,128)(2,1)}, bf16[128,2048]{1,0:T(8,128)(2,1)S(1)}, u32[]{:S(2)}, u32[]{:S(2)}) collective-permute-start(bf16[128,2048]{1,0:T(8,128)(2,1)} %add_convert_fusion.1), channel_id=1, source_target_pairs={{128,192},{129,193},{130,194},{131,195},{132,196},{133,197},{134,1... | collective-permute-start | bytes 1572872 | tf_op jit(solution)/shard_map/ppermute | solution.py:25
  (59 other events, 1137.6 us)
Sparse Core Ops, SparseCore 0:
  10.4 35.3 all-gather.4
  139.1 43.7 all-gather.6
  275.8 46.0 all-gather.8
  432.6 30.8 all-gather.10

commit v4 on v3

--- a/solution.py
+++ b/solution.py
@@ -184,20 +184,50 @@
     )
     tok_pick = tok_match.astype(jnp.bfloat16)
     tok_hit = jnp.any(tok_match, axis=1).reshape(req_count * pair_cap, PAGE)
+    tp_count = lax.axis_size("tp")
+    my_tp = lax.axis_index("tp")
+    gain_own = lax.dynamic_slice_in_dim(gain_full, my_tp * width_loc, width_loc)
+    weight_own = kv_weight[0].reshape(D, 2 * kv_width)
+    relative_rows = [lax.dynamic_slice_in_dim(weight_own, my_tp * width_loc, width_loc, axis=0)]
+    later = [(p * tp_count + t) for p in range(1, section_count) for t in range(tp_count)]
+    for shift in range(1, tp_count):
+        outgoing_rows = lax.dynamic_slice_in_dim(
+            weight_own, ((my_tp + shift) % tp_count) * width_loc, width_loc, axis=0
+        )
+        route = [(i, i - i % tp_count + (i % tp_count + shift) % tp_count) for i in later]
+        relative_rows.append(lax.ppermute(outgoing_rows, ("pipe", "tp"), route))
+    weight_rows = jnp.concatenate(relative_rows, axis=1)
+    block_order = (my_tp - jnp.arange(tp_count, dtype=jnp.int32)) % tp_count
     carried = jnp.zeros((rows_per, width_loc), jnp.bfloat16)
     section_rows = jnp.zeros((RQ * S, width_loc), jnp.bfloat16)
     fresh_rows = jnp.zeros((RQ * S, 2, kv_width), jnp.bfloat16)
     for tick_id in range(batches + section_count - 1):
         offset_batch = tick_id - section_id
         active = (offset_batch >= 0) & (offset_batch < batches)
-        hstate = jnp.where(section_id == 0, hidden, carried)
-        whole_rows = lax.all_gather(hstate, "tp", axis=1, tiled=True)
-        widened = whole_rows.astype(jnp.float32)
-        inv_rms = lax.rsqrt(jnp.mean(widened * widened, axis=-1, keepdims=True) + 1e-05)
-        normed = (widened * inv_rms * gain_full).astype(jnp.bfloat16)
-        projected = jnp.dot(normed, weight_flat, preferred_element_type=jnp.float32).reshape(
-            rows_per, 2, kv_heads, HD
-        )
+        if tick_id == 0:
+            hstate = hidden
+            whole_rows = lax.all_gather(hstate, "tp", axis=1, tiled=True)
+            widened = whole_rows.astype(jnp.float32)
+            inv_rms = lax.rsqrt(jnp.mean(widened * widened, axis=-1, keepdims=True) + 1e-05)
+            normed = (widened * inv_rms * gain_full).astype(jnp.bfloat16)
+            projected = jnp.dot(normed, weight_flat, preferred_element_type=jnp.float32)
+        else:
+            hstate = carried
+            widened = hstate.astype(jnp.float32)
+            scaled = (widened * gain_own).astype(jnp.bfloat16)
+            part_rel = jnp.dot(scaled, weight_rows, preferred_element_type=jnp.float32).reshape(
+                rows_per, tp_count, 2 * kv_width
+            )
+            part_abs = jnp.swapaxes(jnp.take(part_rel, block_order, axis=1), 0, 1)
+            sumsq = jnp.sum(widened * widened, axis=-1)
+            sumsq_rows = jnp.zeros((tp_count, 8, 2 * kv_width), jnp.float32).at[:, 0, :rows_per].set(
+                jnp.broadcast_to(sumsq, (tp_count, rows_per))
+            )
+            got = exchange(jnp.concatenate([part_abs, sumsq_rows], axis=1), "tp", 10 + tick_id)
+            got = jnp.sum(got, axis=0)
+            inv_rms = lax.rsqrt(got[rows_per, :rows_per] / D + 1e-05)
+            projected = got[:rows_per] * inv_rms[:, None]
+        projected = projected.reshape(rows_per, 2, kv_heads, HD)
         new_keys = rotate(projected[:, 0], positions).astype(jnp.bfloat16)
         new_values = projected[:, 1].astype(jnp.bfloat16)
         fresh_kv = jnp.stack(

time: 606 us -> 588 us (0.970)
  waiting for transfers between devices: 84.9 us -> 37.8 us
  Pallas kernels: 265 us -> 296 us
  other arithmetic: 72.3 us -> 61.1 us
  starting transfers between devices: 11.8 us -> 21.7 us
    all_gather x4 -> x1, waiting for transfers between devices: 80.8 us -> 0.01 us  [body(): whole_rows = lax.all_gather(hstate, 'tp', axis=1, tiled=True)]
    ppermute x3, waiting for transfers between devices: 4.03 us -> 37.1 us  [passed_along(): return lax.ppermute(block, axis, [(source, source + 1)])]
    pallas_call x13 -> x16, Pallas kernels: 265 us -> 296 us  [exchange(): pl.pallas_call(functools.partial(exchange_kernel, axis, n, gather, gate),...]
    gather x27, other arithmetic: 32.4 us -> 21.1 us  [body(): box_page[spot_ids // PAGE][:, None]]
    ppermute x0 -> x3, starting transfers between devices: none -> 10.5 us  [body(): relative_rows.append(lax.ppermute(outgoing_rows, ('pipe', 'tp'), route))]
    reduce_sum x4 -> x1, other arithmetic: 8.31 us -> 2.08 us  [body(): jnp.mean(widened * widened, axis=-1, keepdims=True) + 1e-05]
  transfers between devices with their start and end apart: 8 -> 8, of which waited for: 3 -> 1; matrix products, arithmetic and copies ran while one was open for 14% -> 18% of each run, Pallas kernels for 0% -> 10%
where the time goes in v4:
time: 588 us; the launch traced here: 581 us
  Pallas kernels  296 us (50%)
  local copies, waits for them, and re-layouts  99.2 us (17%)
  other arithmetic  61.1 us (10%)
  matrix products  49.1 us (8%)
  waiting for transfers between devices  37.8 us (6%)
  starting transfers between devices  21.7 us (4%)
  between operations  16 us (3%)
    pallas_call x16, Pallas kernels, exchange(): pl.pallas_call(functools.partial(exchange_kernel, axis, n, gather, gate),...  296 us
    ppermute x3, waiting for transfers between devices, passed_along(): return lax.ppermute(block, axis, [(source, source + 1)])  37.1 us
    gather x27, other arithmetic, body(): box_page[spot_ids // PAGE][:, None]  21.1 us
    gather x4, local copies, waits for them, and re-layouts, body(): delta_rows = returned[dest_all, slot_all].reshape(rows_per, width_loc)  12.1 us
  transfers between devices with their start and end apart: 8, of which 1 were waited for; matrix products, arithmetic and copies ran while one was open for 18% of the time, Pallas kernels for 10%

profile of v4, /device:TPU:89, one launch (start us, length us, event | category | flops | bytes accessed | tf_op | source)
XLA Modules:
  0.0 581.1 jit_solution(1256685821965005590)
XLA Ops:
  15.8 8.4 %all-to-all-start = ((s32[16,1,6]{2,1,0:T(1,128)}), s32[16,1,6]{2,1,0:T(1,128)S(1)}, u32[]{:S(2)}, u32[]{:S(2)}) async-start(s32[16,1,6]{2,1,0:T(1,128)} %copy.143), calls=%async_computation | async-start | bytes 16384 | tf_op jit(solution)/shard_map/all_to_all | solution.py:161
  24.3 4.9 copy.194
  36.7 4.4 collective-permute-start.2
  48.2 5.2 gather_fusion.1
  53.4 5.5 copy.137
  67.3 15.4 %select_select_fusion = s32[2048]{0:T(1024)S(1)} fusion(pred[2048]{0:T(1024)(128)(4,1)S(1)} %compare_reduce_fusion, pred[2048]{0:T(1024)(128)(4,1)S(1)} %compare_reduce_fusion.1, pred[2048]{0:T(1024)(128)(4,1)S(1)} %compare_reduce_fusion.2, pred[2048]{0:T(1024)(128)(4,1)S(1)} %compare_reduce_fusion.3, pred[2048]{0:T(1024)(128)(4,1)S(1)} %compare_reduce_fusion.4, ...), kind=kLoop, calls=%fused_computation.301 | loop fusion | flops 51200 | bytes 67684 | tf_op jit(solution)/shard_map/gather | solution.py:182
  86.9 6.4 %copy.138 = bf16[256,8192]{1,0:T(8,128)(2,1)} copy(bf16[256,8192]{0,1:T(8,128)(2,1)} %bitcast.404) | data formatting | bytes 8388608 | tf_op jit(solution)/shard_map/dot_general | solution.py:213
  115.9 19.3 %shard_map.139 = bf16[16,4,4,1024]{3,2,1,0:T(4,128)(2,1)} custom-call(bf16[16,4,4,1024]{3,2,1,0:T(4,128)(2,1)} %copy-done.5), custom_call_target="tpu_custom_call" | custom-call | tf_op jit(solution)/shard_map/pallas_call | solution.py:68
  138.5 9.4 %shard_map.140 = f32[4,256,64]{2,1,0:T(8,128)} custom-call(f32[256,64]{1,0:T(8,128)} %copy.146.x_ref), custom_call_target="tpu_custom_call" | custom-call | tf_op jit(solution)/shard_map/pallas_call | solution.py:68
  151.4 30.8 %shard_map.141 = bf16[16,4,4,2048]{3,2,1,0:T(4,128)(2,1)} custom-call(bf16[16,4,4,2048]{3,2,1,0:T(4,128)(2,1)} %reshape.1619.x_ref), custom_call_target="tpu_custom_call" | custom-call | tf_op jit(solution)/shard_map/pallas_call | solution.py:68
  195.1 10.4 %shard_map.142 = f32[4,136,256]{2,1,0:T(8,128)} custom-call(f32[4,136,256]{2,1,0:T(8,128)} %pad_maximum_fusion.1.x_ref), custom_call_target="tpu_custom_call" | custom-call | tf_op jit(solution)/shard_map/pallas_call | solution.py:68
  217.7 18.7 %shard_map.143 = bf16[16,4,4,1024]{3,2,1,0:T(4,128)(2,1)} custom-call(bf16[16,4,4,1024]{3,2,1,0:T(4,128)(2,1)} %copy-done.6), custom_call_target="tpu_custom_call" | custom-call | tf_op jit(solution)/shard_map/pallas_call | solution.py:68
  239.8 9.4 %shard_map.144 = f32[4,256,64]{2,1,0:T(8,128)} custom-call(f32[256,64]{1,0:T(8,128)} %copy.153.x_ref), custom_call_target="tpu_custom_call" | custom-call | tf_op jit(solution)/shard_map/pallas_call | solution.py:68
  252.2 30.5 %shard_map.145 = bf16[16,4,4,2048]{3,2,1,0:T(4,128)(2,1)} custom-call(bf16[16,4,4,2048]{3,2,1,0:T(4,128)(2,1)} %reshape.1626.x_ref), custom_call_target="tpu_custom_call" | custom-call | tf_op jit(solution)/shard_map/pallas_call | solution.py:68
  297.3 10.4 %shard_map.146 = f32[4,136,256]{2,1,0:T(8,128)} custom-call(f32[4,136,256]{2,1,0:T(8,128)} %pad_maximum_fusion.2.x_ref), custom_call_target="tpu_custom_call" | custom-call | tf_op jit(solution)/shard_map/pallas_call | solution.py:68
  320.6 18.7 %shard_map.147 = bf16[16,4,4,1024]{3,2,1,0:T(4,128)(2,1)} custom-call(bf16[16,4,4,1024]{3,2,1,0:T(4,128)(2,1)} %copy-done.7), custom_call_target="tpu_custom_call" | custom-call | tf_op jit(solution)/shard_map/pallas_call | solution.py:68
  342.6 9.4 %shard_map.148 = f32[4,256,64]{2,1,0:T(8,128)} custom-call(f32[256,64]{1,0:T(8,128)} %copy.160.x_ref), custom_call_target="tpu_custom_call" | custom-call | tf_op jit(solution)/shard_map/pallas_call | solution.py:68
  355.0 30.5 %shard_map.149 = bf16[16,4,4,2048]{3,2,1,0:T(4,128)(2,1)} custom-call(bf16[16,4,4,2048]{3,2,1,0:T(4,128)(2,1)} %reshape.1633.x_ref), custom_call_target="tpu_custom_call" | custom-call | tf_op jit(solution)/shard_map/pallas_call | solution.py:68
  393.4 37.1 %collective-permute-done.5 = bf16[128,2048]{1,0:T(8,128)(2,1)S(1)} collective-permute-done((bf16[128,2048]{1,0:T(8,128)(2,1)S(1)}, bf16[128,2048]{1,0:T(8,128)(2,1)S(1)}, u32[]{:S(2)}, u32[]{:S(2)}) %collective-permute-start.5) | collective-permute-done | bytes 524320 | tf_op jit(solution)/shard_map/ppermute | solution.py:25
  437.1 9.7 %shard_map.150 = f32[4,136,256]{2,1,0:T(8,128)} custom-call(f32[4,136,256]{2,1,0:T(8,128)} %pad_maximum_fusion.3.x_ref), custom_call_target="tpu_custom_call" | custom-call | tf_op jit(solution)/shard_map/pallas_call | solution.py:68
  458.7 30.6 %shard_map.154 = bf16[16,2,2,64,128]{4,3,2,1,0:T(8,128)(2,1)} custom-call(bf16[16,2,2,64,128]{4,3,2,1,0:T(8,128)(2,1)} %bitcast.415), custom_call_target="tpu_custom_call" | custom-call | tf_op jit(solution)/shard_map/pallas_call | solution.py:68
  500.4 18.2 %shard_map.151 = bf16[16,4,4,1024]{3,2,1,0:T(4,128)(2,1)} custom-call(bf16[16,4,4,1024]{3,2,1,0:T(4,128)(2,1)} %copy-done.4), custom_call_target="tpu_custom_call" | custom-call | tf_op jit(solution)/shard_map/pallas_call | solution.py:68
  520.9 9.4 %shard_map.152 = f32[4,256,64]{2,1,0:T(8,128)} custom-call(f32[256,64]{1,0:T(8,128)} %copy.167.x_ref), custom_call_target="tpu_custom_call" | custom-call | tf_op jit(solution)/shard_map/pallas_call | solution.py:68
  533.3 30.5 %shard_map.153 = bf16[16,4,4,2048]{3,2,1,0:T(4,128)(2,1)} custom-call(bf16[16,4,4,2048]{3,2,1,0:T(4,128)(2,1)} %reshape.1640.x_ref), custom_call_target="tpu_custom_call" | custom-call | tf_op jit(solution)/shard_map/pallas_call | solution.py:68
  (374 shorter events, 181.7 us)
Async XLA Ops:
  7.2 142.0 %copy-start = (bf16[1,4,64,2048]{3,2,1,0:T(8,128)(2,1)S(1)}, bf16[1,4,64,2048]{3,2,1,0:T(8,128)(2,1)}, u32[]{:S(2)}) copy-start(bf16[1,4,64,2048]{3,2,1,0:T(8,128)(2,1)} %param.25) | copy-start | bytes 3145732
  7.2 92.5 %all-gather.2.cloned.1.call-start = ((), (), s32[]{:S(2)}) async-start(), calls=%async_computation.1 | async-start | bytes 2621440 | tf_op jit(solution)/shard_map/all_gather | solution.py:209
  15.8 81.3 %all-to-all-start = ((s32[16,1,6]{2,1,0:T(1,128)}), s32[16,1,6]{2,1,0:T(1,128)S(1)}, u32[]{:S(2)}, u32[]{:S(2)}) async-start(s32[16,1,6]{2,1,0:T(1,128)} %copy.143), calls=%async_computation | async-start | bytes 16384 | tf_op jit(solution)/shard_map/all_to_all | solution.py:161
  33.5 156.7 %collective-permute-start.1 = (bf16[2048,256]{1,0:T(8,128)(2,1)}, bf16[2048,256]{1,0:T(8,128)(2,1)}, u32[]{:S(2)}, u32[]{:S(2)}) collective-permute-start(bf16[2048,256]{1,0:T(8,128)(2,1)} %get-tuple-element.61), channel_id=1, source_target_pairs={{64,65},{65,66},{66,67},{67,64},{128,129},{129,130},{130,131},{131... | collective-permute-start | bytes 3145736 | tf_op jit(solution)/shard_map/ppermute | solution.py:198
  36.7 153.6 %collective-permute-start.2 = (bf16[2048,256]{1,0:T(8,128)(2,1)}, bf16[2048,256]{1,0:T(8,128)(2,1)}, u32[]{:S(2)}, u32[]{:S(2)}) collective-permute-start(bf16[2048,256]{1,0:T(8,128)(2,1)} %get-tuple-element.60), channel_id=1, source_target_pairs={{64,66},{65,67},{66,64},{67,65},{128,130},{129,131},{130,128},{131... | collective-permute-start | bytes 3145736 | tf_op jit(solution)/shard_map/ppermute | solution.py:198
  41.0 149.2 %collective-permute-start.3 = (bf16[2048,256]{1,0:T(8,128)(2,1)}, bf16[2048,256]{1,0:T(8,128)(2,1)}, u32[]{:S(2)}, u32[]{:S(2)}) collective-permute-start(bf16[2048,256]{1,0:T(8,128)(2,1)} %get-tuple-element.62), channel_id=1, source_target_pairs={{64,67},{65,64},{66,65},{67,66},{128,131},{129,128},{130,129},{131... | collective-permute-start | bytes 3145736 | tf_op jit(solution)/shard_map/ppermute | solution.py:198
  44.1 61.8 %copy-start.33 = (f32[64]{0:T(128)}, f32[64]{0:T(128)S(1)}, u32[]{:S(2)}) copy-start(f32[64]{0:T(128)S(1)} %multiply_exponential_fusion) | copy-start | bytes 772
  44.1 62.3 %copy-start.46 = (pred[4,4]{1,0:T(4,128)(4,1)}, pred[4,4]{1,0:T(4,128)(4,1)S(1)}, u32[]{:S(2)}) copy-start(pred[4,4]{1,0:T(4,128)(4,1)S(1)} %iota_compare_fusion.6) | copy-start | bytes 52
  45.7 37.0 %copy-start.27 = (s32[2048]{0:T(1024)}, s32[2048]{0:T(1024)S(1)}, u32[]{:S(2)}) copy-start(s32[2048]{0:T(1024)S(1)} %add_select_fusion.1) | copy-start | bytes 24580
  48.0 58.4 %copy-start.15 = (bf16[16,8,8,128]{3,2,1,0:T(8,128)(2,1)}, bf16[16,8,8,128]{3,2,1,0:T(8,128)(2,1)S(1)}, u32[]{:S(2)}) copy-start(bf16[16,8,8,128]{3,2,1,0:T(8,128)(2,1)S(1)} %copy.185) | copy-start | bytes 786436
  63.0 42.9 %copy-start.31 = (f32[128]{0:T(128)}, f32[128]{0:T(128)S(1)}, u32[]{:S(2)}) copy-start(f32[128]{0:T(128)S(1)} %get-tuple-element.76) | copy-start | bytes 1540
  149.7 40.6 %copy-start.35 = (f32[1,2048]{1,0:T(1,128)S(1)}, f32[1,2048]{1,0:T(1,128)}, u32[]{:S(2)}) copy-start(f32[1,2048]{1,0:T(1,128)} %constant_dynamic-slice_fusion.4) | copy-start | bytes 24580
  188.3 1.9 collective-permute-start
  250.9 39.8 %copy-start.36 = (f32[1,2048]{1,0:T(1,128)S(1)}, f32[1,2048]{1,0:T(1,128)}, u32[]{:S(2)}) copy-start(f32[1,2048]{1,0:T(1,128)} %constant_dynamic-slice_fusion.4) | copy-start | bytes 24580
  288.8 1.9 collective-permute-start.4
  390.9 39.6 %collective-permute-start.5 = (bf16[128,2048]{1,0:T(8,128)(2,1)S(1)}, bf16[128,2048]{1,0:T(8,128)(2,1)S(1)}, u32[]{:S(2)}, u32[]{:S(2)}) collective-permute-start(bf16[128,2048]{1,0:T(8,128)(2,1)S(1)} %fusion.42), channel_id=1, source_target_pairs={{128,192},{129,193},{130,194},{131,195},{132,196},{133,197},{134,1... | collective-permute-start | bytes 1572872 | tf_op jit(solution)/shard_map/ppermute | solution.py:25
  393.4 41.5 %copy-start.41 = (pred[4]{0:T(512)(128)(4,1)S(1)}, pred[4]{0:T(512)(128)(4,1)}, u32[]{:S(2)}) copy-start(pred[4]{0:T(512)(128)(4,1)} %compare_and_fusion.2) | copy-start | bytes 16
  452.4 36.9 %copy-start.17 = (bf16[1,128,1,128]{1,3,2,0:T(8,128)(2,1)S(1)}, bf16[1,128,1,128]{1,3,2,0:T(8,128)(2,1)}, u32[]{:S(2)}) copy-start(bf16[1,128,1,128]{1,3,2,0:T(8,128)(2,1)} %slice_bitcast_fusion.22) | copy-start | bytes 98308
  452.4 37.7 %copy-start.16 = (bf16[16,8,8,128]{3,2,1,0:T(8,128)(2,1)S(1)}, bf16[16,8,8,128]{3,2,1,0:T(8,128)(2,1)}, u32[]{:S(2)}) copy-start(bf16[16,8,8,128]{3,2,1,0:T(8,128)(2,1)} %copy-done.15) | copy-start | bytes 786436
  456.1 33.3 %copy-start.23 = (bf16[1,128,1,128]{1,3,2,0:T(8,128)(2,1)S(1)}, bf16[1,128,1,128]{1,3,2,0:T(8,128)(2,1)}, u32[]{:S(2)}) copy-start(bf16[1,128,1,128]{1,3,2,0:T(8,128)(2,1)} %slice_bitcast_fusion.28) | copy-start | bytes 98308
  456.1 34.1 %copy-start.28 = (bf16[128,1,64]{2,0,1:T(8,128)(2,1)S(1)}, bf16[128,1,64]{2,0,1:T(8,128)(2,1)}, u32[]{:S(2)}) copy-start(bf16[128,1,64]{2,0,1:T(8,128)(2,1)} %copy.164) | copy-start | bytes 49156
  456.1 34.1 %copy-start.29 = (bf16[128,1,64]{2,0,1:T(8,128)(2,1)S(1)}, bf16[128,1,64]{2,0,1:T(8,128)(2,1)}, u32[]{:S(2)}) copy-start(bf16[128,1,64]{2,0,1:T(8,128)(2,1)} %copy.165) | copy-start | bytes 49156
  531.6 36.4 %copy-start.3 = (bf16[16,2,2,64,128]{4,3,2,1,0:T(8,128)(2,1)S(1)}, bf16[16,2,2,64,128]{4,3,2,1,0:T(8,128)(2,1)}, u32[]{:S(2)}) copy-start(bf16[16,2,2,64,128]{4,3,2,1,0:T(8,128)(2,1)} %shard_map.154) | copy-start | bytes 3145732
  532.0 37.7 %copy-start.43 = (pred[30]{0:T(512)(128)(4,1)S(1)}, pred[30]{0:T(512)(128)(4,1)}, u32[]{:S(2)}) copy-start(pred[30]{0:T(512)(128)(4,1)} %fusion.135) | copy-start | bytes 94
  (32 other events, 412.4 us)
Sparse Core Ops, SparseCore 0:
  9.8 40.3 all-gather.1

commit v5 on v4

--- a/solution.py
+++ b/solution.py
@@ -171,9 +171,28 @@
     box_move = jnp.argmax(box_match, axis=1)
     box_used = jnp.any(box_match, axis=1)
     box_page = jnp.where(box_used, moves[box_move, 1], -1)
-    out_pages = jnp.where(
-        box_used[:, None, None, None], layer_pages[moves[box_move, 1]], jnp.zeros((), jnp.bfloat16)
-    )
+    box_pick = (box_page[:, None] == jnp.arange(layer_pages.shape[0], dtype=jnp.int32)[None, :]).astype(
+        jnp.bfloat16
+    )
+    land_pick = (spot_match & has_page[:, None]).astype(jnp.bfloat16)
+    box_count = req_count * pair_cap
+
+    def build_pages(fresh):
+        base = jnp.dot(
+            box_pick, layer_pages.reshape(layer_pages.shape[0], -1), preferred_element_type=jnp.float32
+        ).astype(jnp.bfloat16).reshape(box_count, 2, PAGE, kv_width)
+        patch = jnp.dot(
+            tok_pick, fresh.reshape(RQ * S, 2 * kv_width), preferred_element_type=jnp.float32
+        ).astype(jnp.bfloat16)
+        patch = jnp.swapaxes(patch.reshape(box_count, PAGE, 2, kv_width), 1, 2)
+        return jnp.where(tok_hit[:, None, :, None], patch, base).reshape(
+            req_count, pair_cap, 2, PAGE, kv_width
+        )
+
+    def no_pages(fresh):
+        return jnp.zeros((req_count, pair_cap, 2, PAGE, kv_width), jnp.bfloat16)
+
+    arrived = jnp.zeros((free_slots, 2, PAGE, kv_width), jnp.bfloat16)
     page_slot = jnp.take_along_axis(page_table, (positions // PAGE).reshape(RQ, S), axis=1).reshape(
         RQ * S
     )
@@ -223,7 +242,9 @@
             sumsq_rows = jnp.zeros((tp_count, 8, 2 * kv_width), jnp.float32).at[:, 0, :rows_per].set(
                 jnp.broadcast_to(sumsq, (tp_count, rows_per))
             )
-            got = exchange(jnp.concatenate([part_abs, sumsq_rows], axis=1), "tp", 10 + tick_id)
+            got = exchange(
+                jnp.concatenate([part_abs, sumsq_rows], axis=1), "tp", 10 + tick_id, gate=tick_id
+            )
             got = jnp.sum(got, axis=0)
             inv_rms = lax.rsqrt(got[rows_per, :rows_per] / D + 1e-05)
             projected = got[:rows_per] * inv_rms[:, None]
@@ -270,7 +291,7 @@
             .at[dest_all, slot_all]
             .set(attended)
         )
-        rows_in = exchange(outgoing, "req", 0)
+        rows_in = exchange(outgoing, "req", 20 + tick_id, gate=tick_id)
         sources = rows_in.shape[0]
         item_count = rows_in.shape[1]
         flat_rows = rows_in.reshape(sources * item_count * S, q_width)
@@ -282,7 +303,7 @@
         )
         one_hot = (picks_rows[:, None] == adapter_slots[None, :]).astype(jnp.float32)
         partial_low = jnp.sum(all_low * one_hot[:, :, None], axis=1)
-        rank_low = jnp.sum(exchange(partial_low, "tp", 1, gather=True), axis=0).astype(jnp.bfloat16)
+        rank_low = jnp.sum(exchange(partial_low, "tp", 30 + tick_id, gather=True, gate=tick_id), axis=0).astype(jnp.bfloat16)
         spread = (rank_low.astype(jnp.float32)[:, None, :] * one_hot[:, :, None]).astype(
             jnp.bfloat16
         )
@@ -292,7 +313,7 @@
             preferred_element_type=jnp.float32,
         ).astype(jnp.bfloat16)
         deltas = deltas.reshape(sources, item_count, S, width_loc)
-        returned = exchange(deltas, "req", 2)
+        returned = exchange(deltas, "req", 40 + tick_id, gate=tick_id)
         delta_rows = returned[dest_all, slot_all].reshape(rows_per, width_loc)
         new_state = (hstate.astype(jnp.float32) + delta_rows.astype(jnp.float32)).astype(
             jnp.bfloat16
@@ -301,18 +322,15 @@
         fresh_rows = jnp.where(active, fresh_kv, fresh_rows)
         if tick_id + 1 < section_count:
             carried = passed_along(new_state, "pipe", tick_id)
-
-    patch = jnp.dot(
-        tok_pick, fresh_rows.reshape(RQ * S, 2 * kv_width), preferred_element_type=jnp.float32
-    ).astype(jnp.bfloat16)
-    patch = jnp.swapaxes(patch.reshape(req_count * pair_cap, PAGE, 2, kv_width), 1, 2)
-    sent_pages = jnp.where(tok_hit[:, None, :, None], patch, out_pages).reshape(
-        req_count, pair_cap, 2, PAGE, kv_width
-    )
-    got_pages = exchange(sent_pages, "req", 3).reshape(req_count * pair_cap, 2, PAGE, kv_width)
-    arrived = jnp.where(
-        has_page[:, None, None, None], got_pages[page_src], jnp.zeros((), jnp.bfloat16)
-    )
+        sent_pages = lax.cond(section_id == tick_id, build_pages, no_pages, fresh_kv)
+        got_pages = exchange(sent_pages, "req", 50 + tick_id, gate=tick_id)
+        landed = jnp.dot(
+            land_pick, got_pages.reshape(box_count, -1), preferred_element_type=jnp.float32
+        ).astype(jnp.bfloat16)
+        arrived = jnp.where(
+            section_id == tick_id, landed.reshape(free_slots, 2, PAGE, kv_width), arrived
+        )
+
     return (section_rows[None], fresh_rows[None], arrived[None])
 
 

time: 588 us -> 619 us (1.053)
  Pallas kernels: 296 us -> 102 us
  waiting for transfers between devices: 37.8 us -> 194 us
  local copies, waits for them, and re-layouts: 99.2 us -> 138 us
  matrix products: 49.1 us -> 69.7 us
  other arithmetic: 61.1 us -> 67.6 us
    pallas_call x16 -> x19, Pallas kernels: 296 us -> 102 us  [exchange(): pl.pallas_call(functools.partial(exchange_kernel, axis, n, gather, gate),...]
    ppermute x3, waiting for transfers between devices: 37.1 us -> 193 us  [passed_along(): return lax.ppermute(block, axis, [(source, source + 1)])]
    another operation x12 -> x16, local copies, waits for them, and re-layouts: 2.94 us -> 16.1 us
    dot_general x1 -> x6, matrix products: 2.42 us -> 15 us  [the longest x4 10.7 us: body(): jnp.dot(land_pick, got_pages.reshape(box_count, -1), preferred_element_ty...]
    cond x0 -> x5, local copies, waits for them, and re-layouts: none -> 11.1 us  [the longest x4 9.9 us: body(): lax.cond(section_id == tick_id, build_pages, no_pages, fresh_kv)]
    reshape x1 -> x5, local copies, waits for them, and re-layouts: 1.16 us -> 11.5 us  [the longest x4 9.32 us: body(): got_pages.reshape(box_count, -1)]
  transfers between devices with their start and end apart: 8 -> 8, of which waited for: 1 -> 1; matrix products, arithmetic and copies ran while one was open for 18% -> 22% of each run, Pallas kernels for 10% -> 0%
where the time goes in v5:
time: 619 us; the launch traced here: 610 us
  waiting for transfers between devices  194 us (31%)
  local copies, waits for them, and re-layouts  138 us (22%)
  Pallas kernels  102 us (16%)
  matrix products  69.7 us (11%)
  other arithmetic  67.6 us (11%)
  starting transfers between devices  23.2 us (4%)
  between operations  15.9 us (3%)
    ppermute x3, waiting for transfers between devices, passed_along(): return lax.ppermute(block, axis, [(source, source + 1)])  193 us
    pallas_call x19, Pallas kernels, exchange(): pl.pallas_call(functools.partial(exchange_kernel, axis, n, gather, gate),...  102 us
    gather x27, other arithmetic, body(): box_page[spot_ids // PAGE][:, None]  21.1 us
  transfers between devices with their start and end apart: 8, of which 1 were waited for; matrix products, arithmetic and copies ran while one was open for 22% of the time, Pallas kernels for 0%

profile of v5, /device:TPU:89, one launch (start us, length us, event | category | flops | bytes accessed | tf_op | source)
XLA Modules:
  0.0 610.5 jit_solution(8632159267721233715)
XLA Ops:
  15.8 8.4 %all-to-all-start = ((s32[16,1,6]{2,1,0:T(1,128)}), s32[16,1,6]{2,1,0:T(1,128)S(1)}, u32[]{:S(2)}, u32[]{:S(2)}) async-start(s32[16,1,6]{2,1,0:T(1,128)} %copy.191), calls=%async_computation | async-start | bytes 16384 | tf_op jit(solution)/shard_map/all_to_all | solution.py:161
  24.3 4.9 copy.261
  29.2 4.3 constant_dynamic-slice_fusion.3
  33.5 3.1 collective-permute-start.1
  36.7 4.4 collective-permute-start.2
  47.8 5.2 gather_fusion.1
  53.0 5.5 copy.185
  63.5 4.2 compare_select_fusion.2
  67.9 15.6 %select_select_fusion = s32[2048]{0:T(1024)S(1)} fusion(pred[2048]{0:T(1024)(128)(4,1)S(1)} %compare_reduce_fusion, pred[2048]{0:T(1024)(128)(4,1)S(1)} %compare_reduce_fusion.1, pred[2048]{0:T(1024)(128)(4,1)S(1)} %compare_reduce_fusion.2, pred[2048]{0:T(1024)(128)(4,1)S(1)} %compare_reduce_fusion.3, pred[2048]{0:T(1024)(128)(4,1)S(1)} %compare_reduce_fusion.4, ...), kind=kLoop, calls=%fused_computation.319 | loop fusion | flops 51200 | bytes 67684 | tf_op jit(solution)/shard_map/gather | solution.py:201
  87.6 6.4 %copy.186 = bf16[256,8192]{1,0:T(8,128)(2,1)} copy(bf16[256,8192]{0,1:T(8,128)(2,1)} %bitcast.465) | data formatting | bytes 8388608 | tf_op jit(solution)/shard_map/dot_general | solution.py:232
  97.3 4.2 fusion.12
  140.1 4.5 fusion.66
  191.9 3.1 fusion.6
  195.0 4.5 fusion.64
  245.8 3.1 fusion.5
  248.9 193.0 %collective-permute-done.5 = bf16[128,2048]{1,0:T(8,128)(2,1)S(1)} collective-permute-done((bf16[128,2048]{1,0:T(8,128)(2,1)}, bf16[128,2048]{1,0:T(8,128)(2,1)S(1)}, u32[]{:S(2)}, u32[]{:S(2)}) %collective-permute-start.5) | collective-permute-done | bytes 524320 | tf_op jit(solution)/shard_map/ppermute | solution.py:25
  450.1 9.7 %shard_map.150 = f32[4,136,256]{2,1,0:T(8,128)} custom-call(f32[4,136,256]{2,1,0:T(8,128)} %pad_maximum_fusion.3.x_ref), custom_call_target="tpu_custom_call" | custom-call | tf_op jit(solution)/shard_map/pallas_call | solution.py:68
  464.7 21.9 %conditional.4 = (bf16[16,2,2,64,128]{4,2,3,1,0:T(2,128)(2,1)}) conditional(s32[]{:T(128)} %convert_element_type.606, () %tuple.47, (pred[2048]{0:T(1024)(128)(4,1)S(1)}, bf16[128,2,128]{0,2,1:T(8,128)(2,1)S(1)}, bf16[2048,128]{1,0:T(8,128)(2,1)S(1)}, bf16[1,128,2,64,128]{4,3,2,1,0:T(8,128)(2,1)}, bf16[32,128]{1,0:T(8,128)(2,1)S(1)}) %tuple.145), branch_computations={%region_40.42_spmd, %region_41.43_spmd} | conditional | flops 270008320 | bytes 22624264 | solution.py:325
  464.7 7.3 %reshape_squeeze.2 = bf16[128,16384]{1,0:T(8,128)(2,1)} reshape(bf16[1,128,2,64,128]{4,3,2,1,0:T(8,128)(2,1)} %get-tuple-element.93) | data formatting | bytes 8388608 | tf_op jit(solution)/shard_map/cond/branch_1_fun/reshape;squeeze | solution.py:182
  479.8 6.8 %broadcast_select_fusion = bf16[32,2,64,128]{3,1,2,0:T(2,128)(2,1)} fusion(pred[32,64]{1,0:T(8,128)(4,1)S(1)} %broadcast_in_dim.94, bf16[32,64,2,128]{3,2,1,0:T(2,128)(2,1)} %reshape.1639, bf16[32,2,64,128]{3,2,1,0:T(8,128)(2,1)} %bitcast.477), kind=kLoop, calls=%fused_computation.19 | loop fusion | flops 524288 | bytes 3147776 | tf_op jit(solution)/shard_map/cond/branch_1_fun/jit(_where)/select_n | solution.py:188
  489.0 30.8 %shard_map.154 = bf16[16,2,2,64,128]{4,3,2,1,0:T(8,128)(2,1)} custom-call(bf16[16,2,2,64,128]{4,3,2,1,0:T(8,128)(2,1)} %copy.219.x_ref), custom_call_target="tpu_custom_call" | custom-call | tf_op jit(solution)/shard_map/pallas_call | solution.py:68
  535.6 18.2 %shard_map.151 = bf16[16,4,4,1024]{3,2,1,0:T(4,128)(2,1)} custom-call(bf16[16,4,4,1024]{3,2,1,0:T(4,128)(2,1)} %copy-done.3), custom_call_target="tpu_custom_call" | custom-call | tf_op jit(solution)/shard_map/pallas_call | solution.py:68
  557.2 9.5 %shard_map.152 = f32[4,256,64]{2,1,0:T(8,128)} custom-call(f32[256,64]{1,0:T(8,128)} %copy.215.x_ref), custom_call_target="tpu_custom_call" | custom-call | tf_op jit(solution)/shard_map/pallas_call | solution.py:68
  569.5 30.5 %shard_map.153 = bf16[16,4,4,2048]{3,2,1,0:T(4,128)(2,1)} custom-call(bf16[16,4,4,2048]{3,2,1,0:T(4,128)(2,1)} %reshape.1717.x_ref), custom_call_target="tpu_custom_call" | custom-call | tf_op jit(solution)/shard_map/pallas_call | solution.py:68
  (423 shorter events, 213.2 us)
Async XLA Ops:
  7.2 111.8 %copy-start = (bf16[1,4,64,2048]{3,2,1,0:T(8,128)(2,1)S(1)}, bf16[1,4,64,2048]{3,2,1,0:T(8,128)(2,1)}, u32[]{:S(2)}) copy-start(bf16[1,4,64,2048]{3,2,1,0:T(8,128)(2,1)} %param.33) | copy-start | bytes 3145732
  7.2 88.0 %all-gather.2.cloned.1.call-start = ((), (), s32[]{:S(2)}) async-start(), calls=%async_computation.1 | async-start | bytes 2621440 | tf_op jit(solution)/shard_map/all_gather | solution.py:228
  15.8 78.1 %all-to-all-start = ((s32[16,1,6]{2,1,0:T(1,128)}), s32[16,1,6]{2,1,0:T(1,128)S(1)}, u32[]{:S(2)}, u32[]{:S(2)}) async-start(s32[16,1,6]{2,1,0:T(1,128)} %copy.191), calls=%async_computation | async-start | bytes 16384 | tf_op jit(solution)/shard_map/all_to_all | solution.py:161
  29.2 16.1 %copy-start.58 = (s32[32]{0:T(128)S(1)}, s32[32]{0:T(128)}, u32[]{:S(2)}) copy-start(s32[32]{0:T(128)} %param.38) | copy-start | bytes 388
  29.2 16.3 %copy-start.1 = (s32[32,4]{0,1:T(4,128)S(1)}, s32[32,4]{0,1:T(4,128)}, u32[]{:S(2)}) copy-start(s32[32,4]{0,1:T(4,128)} %param.37) | copy-start | bytes 1540
  33.5 106.6 %collective-permute-start.1 = (bf16[2048,256]{1,0:T(8,128)(2,1)}, bf16[2048,256]{1,0:T(8,128)(2,1)}, u32[]{:S(2)}, u32[]{:S(2)}) collective-permute-start(bf16[2048,256]{1,0:T(8,128)(2,1)} %get-tuple-element.231), channel_id=1, source_target_pairs={{64,65},{65,66},{66,67},{67,64},{128,129},{129,130},{130,131},{131... | collective-permute-start | bytes 3145736 | tf_op jit(solution)/shard_map/ppermute | solution.py:217
  36.7 103.4 %collective-permute-start.2 = (bf16[2048,256]{1,0:T(8,128)(2,1)}, bf16[2048,256]{1,0:T(8,128)(2,1)}, u32[]{:S(2)}, u32[]{:S(2)}) collective-permute-start(bf16[2048,256]{1,0:T(8,128)(2,1)} %get-tuple-element.230), channel_id=1, source_target_pairs={{64,66},{65,67},{66,64},{67,65},{128,130},{129,131},{130,128},{131... | collective-permute-start | bytes 3145736 | tf_op jit(solution)/shard_map/ppermute | solution.py:217
  41.0 99.1 %collective-permute-start.3 = (bf16[2048,256]{1,0:T(8,128)(2,1)}, bf16[2048,256]{1,0:T(8,128)(2,1)}, u32[]{:S(2)}, u32[]{:S(2)}) collective-permute-start(bf16[2048,256]{1,0:T(8,128)(2,1)} %get-tuple-element.232), channel_id=1, source_target_pairs={{64,67},{65,64},{66,65},{67,66},{128,131},{129,128},{130,129},{131... | collective-permute-start | bytes 3145736 | tf_op jit(solution)/shard_map/ppermute | solution.py:217
  44.1 57.4 %copy-start.46 = (f32[64]{0:T(128)}, f32[64]{0:T(128)S(1)}, u32[]{:S(2)}) copy-start(f32[64]{0:T(128)S(1)} %multiply_exponential_fusion) | copy-start | bytes 772
  44.1 58.0 %copy-start.59 = (pred[4,4]{1,0:T(4,128)(4,1)}, pred[4,4]{1,0:T(4,128)(4,1)S(1)}, u32[]{:S(2)}) copy-start(pred[4,4]{1,0:T(4,128)(4,1)S(1)} %iota_compare_fusion.7) | copy-start | bytes 52
  47.6 54.6 %copy-start.12 = (bf16[16,8,8,128]{3,2,1,0:T(8,128)(2,1)}, bf16[16,8,8,128]{3,2,1,0:T(8,128)(2,1)S(1)}, u32[]{:S(2)}) copy-start(bf16[16,8,8,128]{3,2,1,0:T(8,128)(2,1)S(1)} %copy.248) | copy-start | bytes 786436
  62.9 38.6 %copy-start.39 = (f32[128]{0:T(128)}, f32[128]{0:T(128)S(1)}, u32[]{:S(2)}) copy-start(f32[128]{0:T(128)S(1)} %get-tuple-element.248) | copy-start | bytes 1540
  95.2 23.8 %copy-start.30 = (f32[256,4]{0,1:T(4,128)}, f32[256,4]{0,1:T(4,128)S(1)}, u32[]{:S(2)}) copy-start(f32[256,4]{0,1:T(4,128)S(1)} %fusion.163) | copy-start | bytes 12292
  127.9 12.2 %collective-permute-start = (bf16[128,2048]{1,0:T(8,128)(2,1)S(1)}, bf16[128,2048]{1,0:T(8,128)(2,1)}, u32[]{:S(2)}, u32[]{:S(2)}) collective-permute-start(bf16[128,2048]{1,0:T(8,128)(2,1)S(1)} %add_convert_fusion), channel_id=1, source_target_pairs={{0,64},{1,65},{2,66},{3,67},{4,68},{5,69},{6,70},{7,71},{8,72},{9,... | collective-permute-start | bytes 1572872 | tf_op jit(solution)/shard_map/ppermute | solution.py:25
  181.4 13.5 %collective-permute-start.4 = (bf16[128,2048]{1,0:T(8,128)(2,1)S(1)}, bf16[128,2048]{1,0:T(8,128)(2,1)}, u32[]{:S(2)}, u32[]{:S(2)}) collective-permute-start(bf16[128,2048]{1,0:T(8,128)(2,1)S(1)} %fusion.47), channel_id=1, source_target_pairs={{64,128},{65,129},{66,130},{67,131},{68,132},{69,133},{70,134},{71... | collective-permute-start | bytes 1572872 | tf_op jit(solution)/shard_map/ppermute | solution.py:25
  236.0 205.9 %collective-permute-start.5 = (bf16[128,2048]{1,0:T(8,128)(2,1)}, bf16[128,2048]{1,0:T(8,128)(2,1)S(1)}, u32[]{:S(2)}, u32[]{:S(2)}) collective-permute-start(bf16[128,2048]{1,0:T(8,128)(2,1)} %fusion.50), channel_id=1, source_target_pairs={{128,192},{129,193},{130,194},{131,195},{132,196},{133,197},{134,1... | collective-permute-start | bytes 1572872 | tf_op jit(solution)/shard_map/ppermute | solution.py:25
  241.7 200.1 %copy-start.54 = (f32[1,2048]{1,0:T(1,128)S(1)}, f32[1,2048]{1,0:T(1,128)}, u32[]{:S(2)}) copy-start(f32[1,2048]{1,0:T(1,128)} %constant_dynamic-slice_fusion.4) | copy-start | bytes 24580
  248.9 199.0 %copy-start.57 = (pred[4]{0:T(512)(128)(4,1)S(1)}, pred[4]{0:T(512)(128)(4,1)}, u32[]{:S(2)}) copy-start(pred[4]{0:T(512)(128)(4,1)} %compare_and_fusion.1) | copy-start | bytes 16
  444.5 17.3 %copy-start.40 = (f32[128]{0:T(128)S(1)}, f32[128]{0:T(128)}, u32[]{:S(2)}) copy-start(f32[128]{0:T(128)} %copy-done.39) | copy-start | bytes 1540
  444.5 17.3 %copy-start.47 = (f32[64]{0:T(128)S(1)}, f32[64]{0:T(128)}, u32[]{:S(2)}) copy-start(f32[64]{0:T(128)} %copy-done.46) | copy-start | bytes 772
  444.5 20.2 %copy-start.35 = (pred[2048]{0:T(1024)(128)(4,1)S(1)}, pred[2048]{0:T(1024)(128)(4,1)}, u32[]{:S(2)}) copy-start(pred[2048]{0:T(1024)(128)(4,1)} %get-tuple-element.244) | copy-start | bytes 6148
  486.6 35.7 %copy-start.45 = (s32[32]{0:T(128)S(1)}, s32[32]{0:T(128)}, u32[]{:S(2)}) copy-start(s32[32]{0:T(128)} %copy-done.41) | copy-start | bytes 388
  486.6 35.7 %copy-start.51 = (pred[30]{0:T(512)(128)(4,1)S(1)}, pred[30]{0:T(512)(128)(4,1)}, u32[]{:S(2)}) copy-start(pred[30]{0:T(512)(128)(4,1)} %fusion.141) | copy-start | bytes 94
  531.2 23.8 %copy-start.31 = (f32[256,4]{0,1:T(4,128)S(1)}, f32[256,4]{0,1:T(4,128)}, u32[]{:S(2)}) copy-start(f32[256,4]{0,1:T(4,128)} %copy-done.30) | copy-start | bytes 12292
  (45 other events, 269.0 us)
Sparse Core Ops, SparseCore 0:
  9.8 40.3 all-gather.1

commit v6 on v5

--- a/solution.py
+++ b/solution.py
@@ -178,6 +178,10 @@
     box_count = req_count * pair_cap
 
     def build_pages(fresh):
+        spot_ids = jnp.arange(req_count * pair_cap * PAGE, dtype=jnp.int32)
+        tok_match = tok_spot[None, :] == spot_ids[:, None]
+        tok_pick = tok_match.astype(jnp.bfloat16)
+        tok_hit = jnp.any(tok_match, axis=1).reshape(req_count * pair_cap, PAGE)
         base = jnp.dot(
             box_pick, layer_pages.reshape(layer_pages.shape[0], -1), preferred_element_type=jnp.float32
         ).astype(jnp.bfloat16).reshape(box_count, 2, PAGE, kv_width)
@@ -196,13 +200,12 @@
     page_slot = jnp.take_along_axis(page_table, (positions // PAGE).reshape(RQ, S), axis=1).reshape(
         RQ * S
     )
-    spot_ids = jnp.arange(req_count * pair_cap * PAGE, dtype=jnp.int32)
-    tok_match = (
-        (page_slot[None, :] == box_page[spot_ids // PAGE][:, None])
-        & ((positions % PAGE)[None, :] == (spot_ids % PAGE)[:, None])
-    )
-    tok_pick = tok_match.astype(jnp.bfloat16)
-    tok_hit = jnp.any(tok_match, axis=1).reshape(req_count * pair_cap, PAGE)
+    tok_in_box = page_slot[:, None] == box_page[None, :]
+    tok_spot = jnp.where(
+        jnp.any(tok_in_box, axis=1),
+        jnp.argmax(tok_in_box, axis=1).astype(jnp.int32) * PAGE + positions % PAGE,
+        -1,
+    )
     tp_count = lax.axis_size("tp")
     my_tp = lax.axis_index("tp")
     gain_own = lax.dynamic_slice_in_dim(gain_full, my_tp * width_loc, width_loc)

time: 619 us -> 587 us (0.948)
  other arithmetic: 67.6 us -> 43.2 us
    gather x28 -> x1, other arithmetic: 21.7 us -> 0.6 us  [the longest x27 21.1 us: body(): box_page[spot_ids // PAGE][:, None]]
  transfers between devices with their start and end apart: 8 -> 8, of which waited for: 1 -> 1; matrix products, arithmetic and copies ran while one was open for 22% -> 18% of each run, Pallas kernels for 0% -> 0%
where the time goes in v6:
time: 587 us; the launch traced here: 581 us
  waiting for transfers between devices  197 us (34%)
  local copies, waits for them, and re-layouts  132 us (22%)
  Pallas kernels  102 us (17%)
  matrix products  66.5 us (11%)
  other arithmetic  43.2 us (7%)
  starting transfers between devices  23.5 us (4%)
  between operations  16.1 us (3%)
    ppermute x3, waiting for transfers between devices, passed_along(): return lax.ppermute(block, axis, [(source, source + 1)])  197 us
    pallas_call x19, Pallas kernels, exchange(): pl.pallas_call(functools.partial(exchange_kernel, axis, n, gather, gate),...  102 us
    dot_general x3, matrix products, body(): jnp.dot(scaled, weight_rows, preferred_element_type=jnp.float32)  13.6 us
  transfers between devices with their start and end apart: 8, of which 1 were waited for; matrix products, arithmetic and copies ran while one was open for 18% of the time, Pallas kernels for 0%

profile of v6, /device:TPU:89, one launch (start us, length us, event | category | flops | bytes accessed | tf_op | source)
XLA Modules:
  0.0 581.1 jit_solution(17995664542110923472)
XLA Ops:
  15.8 8.4 %all-to-all-start = ((s32[16,1,6]{2,1,0:T(1,128)}), s32[16,1,6]{2,1,0:T(1,128)S(1)}, u32[]{:S(2)}, u32[]{:S(2)}) async-start(s32[16,1,6]{2,1,0:T(1,128)} %copy.191), calls=%async_computation | async-start | bytes 16384 | tf_op jit(solution)/shard_map/all_to_all | solution.py:161
  24.3 4.9 copy.261
  29.2 4.3 constant_dynamic-slice_fusion.3
  33.5 3.1 collective-permute-start.1
  36.6 4.4 collective-permute-start.2
  41.0 3.3 collective-permute-start.3
  48.2 5.2 gather_fusion.1
  53.5 5.5 copy.185
  64.3 6.4 %copy.186 = bf16[256,8192]{1,0:T(8,128)(2,1)} copy(bf16[256,8192]{0,1:T(8,128)(2,1)} %bitcast.428) | data formatting | bytes 8388608 | tf_op jit(solution)/shard_map/dot_general | solution.py:235
  73.5 4.2 fusion.20
  95.0 3.0 gather_fusion.2
  112.1 4.5 fusion.72
  138.3 4.6 scatter_fusion.3
  173.9 4.5 fusion.70
  220.2 196.5 %collective-permute-done.5 = bf16[128,2048]{1,0:T(8,128)(2,1)} collective-permute-done((bf16[128,2048]{1,0:T(8,128)(2,1)}, bf16[128,2048]{1,0:T(8,128)(2,1)}, u32[]{:S(2)}, u32[]{:S(2)}) %collective-permute-start.5) | collective-permute-done | bytes 524320 | tf_op jit(solution)/shard_map/ppermute | solution.py:25
  416.7 4.5 fusion.68
  424.2 9.7 %shard_map.150 = f32[4,136,256]{2,1,0:T(8,128)} custom-call(f32[4,136,256]{2,1,0:T(8,128)} %pad_maximum_fusion.3.x_ref), custom_call_target="tpu_custom_call" | custom-call | tf_op jit(solution)/shard_map/pallas_call | solution.py:68
  438.8 18.2 %conditional.4 = (bf16[16,2,2,64,128]{4,2,3,1,0:T(2,128)(2,1)}) conditional(s32[]{:T(128)} %convert_element_type.607, () %tuple.49, (s32[128]{0:T(128)S(1)}, bf16[128,2,128]{0,2,1:T(8,128)(2,1)S(1)}, bf16[1,128,2,64,128]{4,3,2,1,0:T(8,128)(2,1)}, bf16[32,128]{1,0:T(8,128)(2,1)S(1)}) %tuple.114), branch_computations={%region_41.43_spmd, %region_42.45_spmd} | conditional | flops 270792704 | bytes 22103048 | solution.py:328
  442.2 7.3 %reshape_squeeze.2 = bf16[128,16384]{1,0:T(8,128)(2,1)} reshape(bf16[1,128,2,64,128]{4,3,2,1,0:T(8,128)(2,1)} %get-tuple-element.84) | data formatting | bytes 8388608 | tf_op jit(solution)/shard_map/cond/branch_1_fun/reshape;squeeze | solution.py:186
  452.7 4.4 broadcast_select_fusion
  459.6 30.6 %shard_map.154 = bf16[16,2,2,64,128]{4,3,2,1,0:T(8,128)(2,1)} custom-call(bf16[16,2,2,64,128]{4,3,2,1,0:T(8,128)(2,1)} %copy.219.x_ref), custom_call_target="tpu_custom_call" | custom-call | tf_op jit(solution)/shard_map/pallas_call | solution.py:68
  506.0 18.2 %shard_map.151 = bf16[16,4,4,1024]{3,2,1,0:T(4,128)(2,1)} custom-call(bf16[16,4,4,1024]{3,2,1,0:T(4,128)(2,1)} %copy-done.6), custom_call_target="tpu_custom_call" | custom-call | tf_op jit(solution)/shard_map/pallas_call | solution.py:68
  526.5 9.4 %shard_map.152 = f32[4,256,64]{2,1,0:T(8,128)} custom-call(f32[256,64]{1,0:T(8,128)} %copy.215.x_ref), custom_call_target="tpu_custom_call" | custom-call | tf_op jit(solution)/shard_map/pallas_call | solution.py:68
  538.9 30.5 %shard_map.153 = bf16[16,4,4,2048]{3,2,1,0:T(4,128)(2,1)} custom-call(bf16[16,4,4,2048]{3,2,1,0:T(4,128)(2,1)} %reshape.1657.x_ref), custom_call_target="tpu_custom_call" | custom-call | tf_op jit(solution)/shard_map/pallas_call | solution.py:68
  (386 shorter events, 192.9 us)
Async XLA Ops:
  7.2 85.4 %copy-start = (bf16[1,4,64,2048]{3,2,1,0:T(8,128)(2,1)S(1)}, bf16[1,4,64,2048]{3,2,1,0:T(8,128)(2,1)}, u32[]{:S(2)}) copy-start(bf16[1,4,64,2048]{3,2,1,0:T(8,128)(2,1)} %param.33) | copy-start | bytes 3145732
  7.2 64.2 %all-gather.2.cloned.1.call-start = ((), (), s32[]{:S(2)}) async-start(), calls=%async_computation.1 | async-start | bytes 2621440 | tf_op jit(solution)/shard_map/all_gather | solution.py:231
  15.8 54.9 %all-to-all-start = ((s32[16,1,6]{2,1,0:T(1,128)}), s32[16,1,6]{2,1,0:T(1,128)S(1)}, u32[]{:S(2)}, u32[]{:S(2)}) async-start(s32[16,1,6]{2,1,0:T(1,128)} %copy.191), calls=%async_computation | async-start | bytes 16384 | tf_op jit(solution)/shard_map/all_to_all | solution.py:161
  33.5 78.5 %collective-permute-start.1 = (bf16[2048,256]{1,0:T(8,128)(2,1)}, bf16[2048,256]{1,0:T(8,128)(2,1)}, u32[]{:S(2)}, u32[]{:S(2)}) collective-permute-start(bf16[2048,256]{1,0:T(8,128)(2,1)} %get-tuple-element.201), channel_id=1, source_target_pairs={{64,65},{65,66},{66,67},{67,64},{128,129},{129,130},{130,131},{131... | collective-permute-start | bytes 3145736 | tf_op jit(solution)/shard_map/ppermute | solution.py:220
  36.6 75.4 %collective-permute-start.2 = (bf16[2048,256]{1,0:T(8,128)(2,1)}, bf16[2048,256]{1,0:T(8,128)(2,1)}, u32[]{:S(2)}, u32[]{:S(2)}) collective-permute-start(bf16[2048,256]{1,0:T(8,128)(2,1)} %get-tuple-element.200), channel_id=1, source_target_pairs={{64,66},{65,67},{66,64},{67,65},{128,130},{129,131},{130,128},{131... | collective-permute-start | bytes 3145736 | tf_op jit(solution)/shard_map/ppermute | solution.py:220
  41.0 71.1 %collective-permute-start.3 = (bf16[2048,256]{1,0:T(8,128)(2,1)}, bf16[2048,256]{1,0:T(8,128)(2,1)}, u32[]{:S(2)}, u32[]{:S(2)}) collective-permute-start(bf16[2048,256]{1,0:T(8,128)(2,1)} %get-tuple-element.202), channel_id=1, source_target_pairs={{64,67},{65,64},{66,65},{67,66},{128,131},{129,128},{130,129},{131... | collective-permute-start | bytes 3145736 | tf_op jit(solution)/shard_map/ppermute | solution.py:220
  48.0 30.2 %copy-start.12 = (bf16[16,8,8,128]{3,2,1,0:T(8,128)(2,1)}, bf16[16,8,8,128]{3,2,1,0:T(8,128)(2,1)S(1)}, u32[]{:S(2)}) copy-start(bf16[16,8,8,128]{3,2,1,0:T(8,128)(2,1)S(1)} %copy.248) | copy-start | bytes 786436
  59.0 18.7 %copy-start.40 = (f32[64]{0:T(128)}, f32[64]{0:T(128)S(1)}, u32[]{:S(2)}) copy-start(f32[64]{0:T(128)S(1)} %multiply_exponential_fusion) | copy-start | bytes 772
  59.0 19.2 %copy-start.55 = (pred[4,4]{1,0:T(4,128)(4,1)}, pred[4,4]{1,0:T(4,128)(4,1)S(1)}, u32[]{:S(2)}) copy-start(pred[4,4]{1,0:T(4,128)(4,1)S(1)} %iota_compare_fusion.15) | copy-start | bytes 52
  61.1 16.6 %copy-start.37 = (f32[128]{0:T(128)}, f32[128]{0:T(128)S(1)}, u32[]{:S(2)}) copy-start(f32[128]{0:T(128)S(1)} %get-tuple-element.216) | copy-start | bytes 1540
  61.1 41.6 %copy-start.27 = (s32[128]{0:T(128)}, s32[128]{0:T(128)S(1)}, u32[]{:S(2)}) copy-start(s32[128]{0:T(128)S(1)} %get-tuple-element.215) | copy-start | bytes 1540
  71.2 39.1 %copy-start.33 = (s32[32]{0:T(128)}, s32[32]{0:T(128)S(1)}, u32[]{:S(2)}) copy-start(s32[32]{0:T(128)S(1)} %eq.140) | copy-start | bytes 388
  71.4 39.0 %copy-start.43 = (pred[30]{0:T(512)(128)(4,1)}, pred[30]{0:T(512)(128)(4,1)S(1)}, u32[]{:S(2)}) copy-start(pred[30]{0:T(512)(128)(4,1)S(1)} %fusion.147) | copy-start | bytes 94
  71.4 21.2 %copy-start.23 = (f32[256,4]{0,1:T(4,128)}, f32[256,4]{0,1:T(4,128)S(1)}, u32[]{:S(2)}) copy-start(f32[256,4]{0,1:T(4,128)S(1)} %fusion.166) | copy-start | bytes 12292
  101.1 11.0 %collective-permute-start = (bf16[128,2048]{1,0:T(8,128)(2,1)}, bf16[128,2048]{1,0:T(8,128)(2,1)}, u32[]{:S(2)}, u32[]{:S(2)}) collective-permute-start(bf16[128,2048]{1,0:T(8,128)(2,1)} %add_convert_fusion), channel_id=1, source_target_pairs={{0,64},{1,65},{2,66},{3,67},{4,68},{5,69},{6,70},{7,71},{8,72},{9,... | collective-permute-start | bytes 1572872 | tf_op jit(solution)/shard_map/ppermute | solution.py:25
  161.0 12.8 %collective-permute-start.4 = (bf16[128,2048]{1,0:T(8,128)(2,1)}, bf16[128,2048]{1,0:T(8,128)(2,1)}, u32[]{:S(2)}, u32[]{:S(2)}) collective-permute-start(bf16[128,2048]{1,0:T(8,128)(2,1)} %fusion.55), channel_id=1, source_target_pairs={{64,128},{65,129},{66,130},{67,131},{68,132},{69,133},{70,134},{71... | collective-permute-start | bytes 1572872 | tf_op jit(solution)/shard_map/ppermute | solution.py:25
  208.3 208.4 %collective-permute-start.5 = (bf16[128,2048]{1,0:T(8,128)(2,1)}, bf16[128,2048]{1,0:T(8,128)(2,1)}, u32[]{:S(2)}, u32[]{:S(2)}) collective-permute-start(bf16[128,2048]{1,0:T(8,128)(2,1)} %fusion.58), channel_id=1, source_target_pairs={{128,192},{129,193},{130,194},{131,195},{132,196},{133,197},{134,1... | collective-permute-start | bytes 1572872 | tf_op jit(solution)/shard_map/ppermute | solution.py:25
  214.2 202.6 %copy-start.49 = (f32[1,2048]{1,0:T(1,128)S(1)}, f32[1,2048]{1,0:T(1,128)}, u32[]{:S(2)}) copy-start(f32[1,2048]{1,0:T(1,128)} %constant_dynamic-slice_fusion.4) | copy-start | bytes 24580
  220.2 201.8 %copy-start.52 = (pred[4]{0:T(512)(128)(4,1)S(1)}, pred[4]{0:T(512)(128)(4,1)}, u32[]{:S(2)}) copy-start(pred[4]{0:T(512)(128)(4,1)} %compare_and_fusion) | copy-start | bytes 16
  457.0 35.5 %copy-start.4 = (bf16[30,16384]{1,0:T(8,128)(2,1)S(1)}, bf16[30,16384]{1,0:T(8,128)(2,1)}, u32[]{:S(2)}) copy-start(bf16[30,16384]{1,0:T(8,128)(2,1)} %fusion.13) | copy-start | bytes 2949124
  457.1 35.5 %copy-start.36 = (s32[32]{0:T(128)S(1)}, s32[32]{0:T(128)}, u32[]{:S(2)}) copy-start(s32[32]{0:T(128)} %copy-done.33) | copy-start | bytes 388
  457.1 35.5 %copy-start.46 = (pred[30]{0:T(512)(128)(4,1)S(1)}, pred[30]{0:T(512)(128)(4,1)}, u32[]{:S(2)}) copy-start(pred[30]{0:T(512)(128)(4,1)} %copy-done.43) | copy-start | bytes 94
  501.6 23.9 %copy-start.25 = (f32[256,4]{0,1:T(4,128)S(1)}, f32[256,4]{0,1:T(4,128)}, u32[]{:S(2)}) copy-start(f32[256,4]{0,1:T(4,128)} %copy-done.23) | copy-start | bytes 12292
  501.6 23.9 %copy-start.54 = (bf16[1,4,64,1024]{3,2,1,0:T(8,128)(2,1)S(1)}, bf16[1,4,64,1024]{3,2,1,0:T(8,128)(2,1)}, u32[]{:S(2)}) copy-start(bf16[1,4,64,1024]{3,2,1,0:T(8,128)(2,1)} %param.32) | copy-start | bytes 1572868
  (40 other events, 236.2 us)
Sparse Core Ops, SparseCore 0:
  9.8 40.3 all-gather.1

commit v7 on v6

--- a/solution.py
+++ b/solution.py
@@ -177,14 +177,22 @@
     land_pick = (spot_match & has_page[:, None]).astype(jnp.bfloat16)
     box_count = req_count * pair_cap
 
+    def build_base():
+        return jnp.dot(
+            box_pick, layer_pages.reshape(layer_pages.shape[0], -1), preferred_element_type=jnp.float32
+        ).astype(jnp.bfloat16).reshape(box_count, 2, PAGE, kv_width)
+
+    def no_base():
+        return jnp.zeros((box_count, 2, PAGE, kv_width), jnp.bfloat16)
+
+    base_early = lax.cond(section_id != 0, build_base, no_base)
+
     def build_pages(fresh):
         spot_ids = jnp.arange(req_count * pair_cap * PAGE, dtype=jnp.int32)
         tok_match = tok_spot[None, :] == spot_ids[:, None]
         tok_pick = tok_match.astype(jnp.bfloat16)
         tok_hit = jnp.any(tok_match, axis=1).reshape(req_count * pair_cap, PAGE)
-        base = jnp.dot(
-            box_pick, layer_pages.reshape(layer_pages.shape[0], -1), preferred_element_type=jnp.float32
-        ).astype(jnp.bfloat16).reshape(box_count, 2, PAGE, kv_width)
+        base = lax.cond(section_id == 0, build_base, lambda: base_early)
         patch = jnp.dot(
             tok_pick, fresh.reshape(RQ * S, 2 * kv_width), preferred_element_type=jnp.float32
         ).astype(jnp.bfloat16)

time: 587 us -> 611 us (1.041)
  local copies, waits for them, and re-layouts: 132 us -> 148 us
  matrix products: 66.5 us -> 75.1 us
    cond x5 -> x1, local copies, waits for them, and re-layouts: 10.3 us -> 0.24 us  [the longest x4 10.1 us: body(): lax.cond(section_id == tick_id, build_pages, no_pages, fresh_kv)]
  transfers between devices with their start and end apart: 8 -> 8, of which waited for: 1 -> 1; matrix products, arithmetic and copies ran while one was open for 18% -> 20% of each run, Pallas kernels for 0% -> 0%
where the time goes in v7:
time: 611 us; the launch traced here: 601 us
  waiting for transfers between devices  195 us (32%)
  local copies, waits for them, and re-layouts  148 us (24%)
  Pallas kernels  102 us (17%)
  matrix products  75.1 us (12%)
  other arithmetic  43.7 us (7%)
  starting transfers between devices  22 us (4%)
  between operations  15.6 us (3%)
    ppermute x3, waiting for transfers between devices, passed_along(): return lax.ppermute(block, axis, [(source, source + 1)])  194 us
    pallas_call x19, Pallas kernels, exchange(): pl.pallas_call(functools.partial(exchange_kernel, axis, n, gather, gate),...  102 us
    scatter x4, local copies, waits for them, and re-layouts, body(): outgoing = jnp.zeros((req_count, batch_cap, S, q_width), jnp.bfloat16).at...  15.8 us
    dot_general x3, matrix products, body(): jnp.dot(scaled, weight_rows, preferred_element_type=jnp.float32)  13.6 us
  transfers between devices with their start and end apart: 8, of which 1 were waited for; matrix products, arithmetic and copies ran while one was open for 20% of the time, Pallas kernels for 0%

profile of v7, /device:TPU:89, one launch (start us, length us, event | category | flops | bytes accessed | tf_op | source)
XLA Modules:
  0.0 601.4 jit_solution(2709546038373136876)
XLA Ops:
  15.8 8.4 %all-to-all-start = ((s32[16,1,6]{2,1,0:T(1,128)}), s32[16,1,6]{2,1,0:T(1,128)S(1)}, u32[]{:S(2)}, u32[]{:S(2)}) async-start(s32[16,1,6]{2,1,0:T(1,128)} %copy.175), calls=%async_computation | async-start | bytes 16384 | tf_op jit(solution)/shard_map/all_to_all | solution.py:161
  24.3 4.9 copy.242
  29.2 4.3 constant_dynamic-slice_fusion.3
  33.5 4.4 collective-permute-start.3
  43.1 5.2 gather_fusion.1
  48.4 5.6 copy.169
  63.4 6.4 %copy.170 = bf16[256,8192]{1,0:T(8,128)(2,1)} copy(bf16[256,8192]{0,1:T(8,128)(2,1)} %bitcast.436) | data formatting | bytes 8388608 | tf_op jit(solution)/shard_map/dot_general | solution.py:243
  69.8 10.6 %conditional.9 = (bf16[32,2,64,128]{3,2,1,0:T(8,128)(2,1)S(1)}) conditional(s32[]{:T(128)} %convert_element_type.627, () %tuple.80, (bf16[1,128,2,64,128]{4,3,2,1,0:T(8,128)(2,1)}, bf16[32,128]{1,0:T(8,128)(2,1)S(1)}) %tuple.81), branch_computations={%region_41.43_spmd, %region_42.44_spmd} | conditional | flops 134742016 | bytes 15736840 | solution.py:188
  69.8 7.3 %reshape_squeeze.4 = bf16[128,16384]{1,0:T(8,128)(2,1)} reshape(bf16[1,128,2,64,128]{4,3,2,1,0:T(8,128)(2,1)} %get-tuple-element.137) | data formatting | bytes 8388608 | tf_op jit(solution)/shard_map/cond/branch_1_fun/reshape;squeeze | solution.py:182
  84.4 4.2 fusion.21
  101.8 4.6 scatter_fusion
  134.7 4.5 fusion.73
  159.6 4.6 scatter_fusion.3
  188.8 3.1 fusion.15
  193.2 4.5 fusion.71
  218.0 4.6 scatter_fusion.4
  249.5 193.8 %collective-permute-done.5 = bf16[128,2048]{1,0:T(8,128)(2,1)} collective-permute-done((bf16[128,2048]{1,0:T(8,128)(2,1)}, bf16[128,2048]{1,0:T(8,128)(2,1)}, u32[]{:S(2)}, u32[]{:S(2)}) %collective-permute-start.5) | collective-permute-done | bytes 524320 | tf_op jit(solution)/shard_map/ppermute | solution.py:25
  444.5 4.5 fusion.69
  454.5 9.7 %shard_map.150 = f32[4,136,256]{2,1,0:T(8,128)} custom-call(f32[4,136,256]{2,1,0:T(8,128)} %pad_maximum_fusion.3.x_ref), custom_call_target="tpu_custom_call" | custom-call | tf_op jit(solution)/shard_map/pallas_call | solution.py:68
  479.8 19.3 %shard_map.151 = bf16[16,4,4,1024]{3,2,1,0:T(4,128)(2,1)} custom-call(bf16[16,4,4,1024]{3,2,1,0:T(4,128)(2,1)} %copy-done.4), custom_call_target="tpu_custom_call" | custom-call | tf_op jit(solution)/shard_map/pallas_call | solution.py:68
  502.5 9.4 %shard_map.152 = f32[4,256,64]{2,1,0:T(8,128)} custom-call(f32[256,64]{1,0:T(8,128)} %copy.199.x_ref), custom_call_target="tpu_custom_call" | custom-call | tf_op jit(solution)/shard_map/pallas_call | solution.py:68
  514.9 30.5 %shard_map.153 = bf16[16,4,4,2048]{3,2,1,0:T(4,128)(2,1)} custom-call(bf16[16,4,4,2048]{3,2,1,0:T(4,128)(2,1)} %reshape.1660.x_ref), custom_call_target="tpu_custom_call" | custom-call | tf_op jit(solution)/shard_map/pallas_call | solution.py:68
  551.2 6.4 %conditional.10 = (bf16[16,2,2,64,128]{4,3,2,1,0:T(8,128)(2,1)}) conditional(s32[]{:T(128)} %convert_element_type.625, () %tuple.79, (s32[128]{0:T(128)S(1)}, bf16[128,2,128]{0,2,1:T(8,128)(2,1)S(1)}, s32[]{:T(128)}, bf16[32,2,64,128]{3,2,1,0:T(8,128)(2,1)S(1)}, bf16[1,128,2,64,128]{4,3,2,1,0:T(8,128)(2,1)}, ...), branch_computations={%region_43.45_spmd, %region_44.49_spmd} | conditional | flops 270792704 | bytes 22103086 | solution.py:336
  557.6 29.5 %shard_map.154 = bf16[16,2,2,64,128]{4,3,2,1,0:T(8,128)(2,1)} custom-call(bf16[16,2,2,64,128]{4,3,2,1,0:T(8,128)(2,1)} %get-tuple-element.351.x_ref), custom_call_target="tpu_custom_call" | custom-call | tf_op jit(solution)/shard_map/pallas_call | solution.py:68
  (348 shorter events, 215.8 us)
Async XLA Ops:
  7.2 105.2 %copy-start = (bf16[1,4,64,2048]{3,2,1,0:T(8,128)(2,1)S(1)}, bf16[1,4,64,2048]{3,2,1,0:T(8,128)(2,1)}, u32[]{:S(2)}) copy-start(bf16[1,4,64,2048]{3,2,1,0:T(8,128)(2,1)} %param.43) | copy-start | bytes 3145732
  7.2 75.1 %all-gather.2.cloned.1.call-start = ((), (), s32[]{:S(2)}) async-start(), calls=%async_computation.1 | async-start | bytes 2621440 | tf_op jit(solution)/shard_map/all_gather | solution.py:239
  15.8 64.5 %all-to-all-start = ((s32[16,1,6]{2,1,0:T(1,128)}), s32[16,1,6]{2,1,0:T(1,128)S(1)}, u32[]{:S(2)}, u32[]{:S(2)}) async-start(s32[16,1,6]{2,1,0:T(1,128)} %copy.175), calls=%async_computation | async-start | bytes 16384 | tf_op jit(solution)/shard_map/all_to_all | solution.py:161
  29.2 13.7 %copy-start.2 = (s32[16,3]{0,1:T(4,128)S(1)}, s32[16,3]{0,1:T(4,128)}, u32[]{:S(2)}) copy-start(s32[16,3]{0,1:T(4,128)} %param.49) | copy-start | bytes 580
  29.2 13.7 %copy-start.1 = (s32[32,4]{0,1:T(4,128)S(1)}, s32[32,4]{0,1:T(4,128)}, u32[]{:S(2)}) copy-start(s32[32,4]{0,1:T(4,128)} %param.47) | copy-start | bytes 1540
  33.5 101.1 %collective-permute-start.3 = (bf16[2048,256]{1,0:T(8,128)(2,1)}, bf16[2048,256]{1,0:T(8,128)(2,1)}, u32[]{:S(2)}, u32[]{:S(2)}) collective-permute-start(bf16[2048,256]{1,0:T(8,128)(2,1)} %get-tuple-element.315), channel_id=1, source_target_pairs={{64,67},{65,64},{66,65},{67,66},{128,131},{129,128},{130,129},{131... | collective-permute-start | bytes 3145736 | tf_op jit(solution)/shard_map/ppermute | solution.py:228
  37.9 96.8 %collective-permute-start.2 = (bf16[2048,256]{1,0:T(8,128)(2,1)}, bf16[2048,256]{1,0:T(8,128)(2,1)}, u32[]{:S(2)}, u32[]{:S(2)}) collective-permute-start(bf16[2048,256]{1,0:T(8,128)(2,1)} %get-tuple-element.313), channel_id=1, source_target_pairs={{64,66},{65,67},{66,64},{67,65},{128,130},{129,131},{130,128},{131... | collective-permute-start | bytes 3145736 | tf_op jit(solution)/shard_map/ppermute | solution.py:228
  40.3 94.3 %collective-permute-start.1 = (bf16[2048,256]{1,0:T(8,128)(2,1)}, bf16[2048,256]{1,0:T(8,128)(2,1)}, u32[]{:S(2)}, u32[]{:S(2)}) collective-permute-start(bf16[2048,256]{1,0:T(8,128)(2,1)} %get-tuple-element.314), channel_id=1, source_target_pairs={{64,65},{65,66},{66,67},{67,64},{128,129},{129,130},{130,131},{131... | collective-permute-start | bytes 3145736 | tf_op jit(solution)/shard_map/ppermute | solution.py:228
  54.0 36.6 %copy-start.12 = (bf16[16,8,8,128]{3,2,1,0:T(8,128)(2,1)}, bf16[16,8,8,128]{3,2,1,0:T(8,128)(2,1)S(1)}, u32[]{:S(2)}) copy-start(bf16[16,8,8,128]{3,2,1,0:T(8,128)(2,1)S(1)} %copy.229) | copy-start | bytes 786436
  113.9 11.5 %copy-start.14 = (f32[128,2,128]{0,2,1:T(8,128)S(1)}, f32[128,2,128]{0,2,1:T(8,128)}, u32[]{:S(2)}) copy-start(f32[128,2,128]{0,2,1:T(8,128)} %copy-done.13) | copy-start | bytes 393220
  123.8 9.6 %collective-permute-start = (bf16[128,2048]{1,0:T(8,128)(2,1)}, bf16[128,2048]{1,0:T(8,128)(2,1)}, u32[]{:S(2)}, u32[]{:S(2)}) collective-permute-start(bf16[128,2048]{1,0:T(8,128)(2,1)} %add_convert_fusion), channel_id=1, source_target_pairs={{0,64},{1,65},{2,66},{3,67},{4,68},{5,69},{6,70},{7,71},{8,72},{9,... | collective-permute-start | bytes 1572872 | tf_op jit(solution)/shard_map/ppermute | solution.py:25
  171.6 11.4 %copy-start.23 = (bf16[128,1,128]{0,2,1:T(8,128)(2,1)S(1)}, bf16[128,1,128]{0,2,1:T(8,128)(2,1)}, u32[]{:S(2)}) copy-start(bf16[128,1,128]{0,2,1:T(8,128)(2,1)} %slice_bitcast_fusion.23) | copy-start | bytes 98308
  181.5 10.4 %collective-permute-start.4 = (bf16[128,2048]{1,0:T(8,128)(2,1)}, bf16[128,2048]{1,0:T(8,128)(2,1)}, u32[]{:S(2)}, u32[]{:S(2)}) collective-permute-start(bf16[128,2048]{1,0:T(8,128)(2,1)} %fusion.56), channel_id=1, source_target_pairs={{64,128},{65,129},{66,130},{67,131},{68,132},{69,133},{70,134},{71... | collective-permute-start | bytes 1572872 | tf_op jit(solution)/shard_map/ppermute | solution.py:25
  204.5 9.2 %copy-start.6 = (f32[128,256]{0,1:T(8,128)}, f32[128,256]{0,1:T(8,128)S(1)}, u32[]{:S(2)}) copy-start(f32[128,256]{0,1:T(8,128)S(1)} %copy.188) | copy-start | bytes 393220
  230.0 11.2 %copy-start.24 = (bf16[128,1,128]{0,2,1:T(8,128)(2,1)S(1)}, bf16[128,1,128]{0,2,1:T(8,128)(2,1)}, u32[]{:S(2)}) copy-start(bf16[128,1,128]{0,2,1:T(8,128)(2,1)} %slice_bitcast_fusion.25) | copy-start | bytes 98308
  240.0 203.3 %collective-permute-start.5 = (bf16[128,2048]{1,0:T(8,128)(2,1)}, bf16[128,2048]{1,0:T(8,128)(2,1)}, u32[]{:S(2)}, u32[]{:S(2)}) collective-permute-start(bf16[128,2048]{1,0:T(8,128)(2,1)} %fusion.59), channel_id=1, source_target_pairs={{128,192},{129,193},{130,194},{131,195},{132,196},{133,197},{134,1... | collective-permute-start | bytes 1572872 | tf_op jit(solution)/shard_map/ppermute | solution.py:25
  242.7 201.8 %copy-start.32 = (f32[1,2048]{1,0:T(1,128)S(1)}, f32[1,2048]{1,0:T(1,128)}, u32[]{:S(2)}) copy-start(f32[1,2048]{1,0:T(1,128)} %constant_dynamic-slice_fusion.4) | copy-start | bytes 24580
  513.2 36.4 %copy-start.15 = (bf16[1,128,1,128]{1,3,2,0:T(8,128)(2,1)S(1)}, bf16[1,128,1,128]{1,3,2,0:T(8,128)(2,1)}, u32[]{:S(2)}) copy-start(bf16[1,128,1,128]{1,3,2,0:T(8,128)(2,1)} %maximum_bitcast_fusion.11) | copy-start | bytes 98308
  513.2 36.4 %copy-start.16 = (bf16[1,128,1,128]{1,3,2,0:T(8,128)(2,1)S(1)}, bf16[1,128,1,128]{1,3,2,0:T(8,128)(2,1)}, u32[]{:S(2)}) copy-start(bf16[1,128,1,128]{1,3,2,0:T(8,128)(2,1)} %slice_bitcast_fusion.22) | copy-start | bytes 98308
  513.2 36.4 %copy-start.17 = (bf16[1,128,1,128]{1,3,2,0:T(8,128)(2,1)S(1)}, bf16[1,128,1,128]{1,3,2,0:T(8,128)(2,1)}, u32[]{:S(2)}) copy-start(bf16[1,128,1,128]{1,3,2,0:T(8,128)(2,1)} %maximum_bitcast_fusion.10) | copy-start | bytes 98308
  513.2 36.4 %copy-start.18 = (bf16[1,128,1,128]{1,3,2,0:T(8,128)(2,1)S(1)}, bf16[1,128,1,128]{1,3,2,0:T(8,128)(2,1)}, u32[]{:S(2)}) copy-start(bf16[1,128,1,128]{1,3,2,0:T(8,128)(2,1)} %slice_bitcast_fusion.24) | copy-start | bytes 98308
  513.2 36.4 %copy-start.19 = (bf16[1,128,1,128]{1,3,2,0:T(8,128)(2,1)S(1)}, bf16[1,128,1,128]{1,3,2,0:T(8,128)(2,1)}, u32[]{:S(2)}) copy-start(bf16[1,128,1,128]{1,3,2,0:T(8,128)(2,1)} %maximum_bitcast_fusion.9) | copy-start | bytes 98308
  513.2 36.4 %copy-start.20 = (bf16[1,128,1,128]{1,3,2,0:T(8,128)(2,1)S(1)}, bf16[1,128,1,128]{1,3,2,0:T(8,128)(2,1)}, u32[]{:S(2)}) copy-start(bf16[1,128,1,128]{1,3,2,0:T(8,128)(2,1)} %slice_bitcast_fusion.28) | copy-start | bytes 98308
  557.6 31.8 %copy-start.3 = (bf16[30,16384]{1,0:T(8,128)(2,1)S(1)}, bf16[30,16384]{1,0:T(8,128)(2,1)}, u32[]{:S(2)}) copy-start(bf16[30,16384]{1,0:T(8,128)(2,1)} %fusion.14) | copy-start | bytes 2949124
  (22 other events, 90.6 us)
Sparse Core Ops, SparseCore 0:
  9.8 39.7 all-gather.1
